TPU v7x, 32 devices: a whole 2x2x4 slice. The times are simulated.
32 devices in a mesh: fsdp: 8 (over z, y), ctx: 4 (over x, core).
Axes of the slice: x: 2, y: 2, z: 4, core: 2. Of those that a mesh axis runs over, the one named last changes fastest.
Arguments:
- tokens: bfloat16 [2, 8, 512, 512], P(None, 'fsdp', 'ctx'), may hold values from -6 to 6
- lengths: int32 [2, 8], P(None, 'fsdp'), may hold values from 8 to 512, as said below
- cotangent: bfloat16 [2, 8, 512, 512], P(None, 'fsdp', 'ctx'), may hold values from -6 to 6
- first_up: bfloat16 [512, 2048], P('fsdp'), may hold values from -0.25 to 0.25
- first_down: bfloat16 [2048, 512], P('fsdp'), may hold values from -0.125 to 0.125
- project_in: bfloat16 [512, 1536], P('fsdp'), may hold values from -0.25 to 0.25
- project_out: bfloat16 [512, 512], P('fsdp'), may hold values from -1 to 1
- pointwise_in: bfloat16 [512, 1024], P('fsdp'), may hold values from -0.25 to 0.25
- depthwise: bfloat16 [512, 31], P('fsdp'), may hold values from -1 to 1
- pointwise_out: bfloat16 [512, 512], P('fsdp'), may hold values from -0.25 to 0.25
- second_up: bfloat16 [512, 2048], P('fsdp'), may hold values from -0.25 to 0.25
- second_down: bfloat16 [2048, 512], P('fsdp'), may hold values from -0.125 to 0.125
- gains: bfloat16 [6, 512], P(None, 'fsdp'), may hold values from 0.25 to 1.75
- batch_shift: bfloat16 [512], P('fsdp'), may hold values from -3 to 3
- head_terms: float32 [2, 8], replicated, may hold values from -3 to 300, as said below
Outputs:
- output: bfloat16 [2, 8, 512, 512], P(None, 'fsdp', 'ctx')
- grad_tokens: bfloat16 [2, 8, 512, 512], P(None, 'fsdp', 'ctx')
- grad_first_up: float32 [512, 2048], P('fsdp')
- grad_first_down: float32 [2048, 512], P('fsdp')
- grad_project_in: float32 [512, 1536], P('fsdp')
- grad_project_out: float32 [512, 512], P('fsdp')
- grad_pointwise_in: float32 [512, 1024], P('fsdp')
- grad_depthwise: float32 [512, 31], P('fsdp')
- grad_pointwise_out: float32 [512, 512], P('fsdp')
- grad_second_up: float32 [512, 2048], P('fsdp')
- grad_second_down: float32 [2048, 512], P('fsdp')
- grad_gains: float32 [6, 512], P(None, 'fsdp')
- grad_batch_shift: float32 [512], P('fsdp')
- grad_head_terms: float32 [2, 8], replicated
Inputs may be any that keep to these rules, and one draw needn't show every extreme that they name: `lengths`: the first sequence of every micro-batch has all 512 frames. `head_terms`: row 0 is positive.
All inputs are finite; a program needn't handle non-finite values.
Results may differ from a plain program's by a relative error of at most 0.02.
Values may be sent and summed in bfloat16 or wider, within the bound.
A program may use at most 128 MiB of HBM per device.

v0:
```python
import jax
import jax.numpy as jnp
from jax import lax
from jax.sharding import PartitionSpec as P

H = 8
HD = 64
RFAR = 256


EPS = 1e-05
NEGATIVE = -1e30


def extended(block, sides, width):
    for axis, dim in sides:
        count = lax.axis_size(axis)
        forward = [(i, i + 1) for i in range(count - 1)]
        backward = [(target, source) for source, target in forward]
        low = lax.ppermute(
            lax.slice_in_dim(block, block.shape[dim] - width, None, axis=dim), axis, forward
        )
        high = lax.ppermute(lax.slice_in_dim(block, 0, width, axis=dim), axis, backward)
        block = jnp.concatenate([low, block, high], axis=dim)
    return block


def product(left, right):
    return jnp.dot(left, right, preferred_element_type=jnp.float32)


def product_left(left, right):
    return jnp.dot(left.T, right, preferred_element_type=jnp.float32)


def product_right(left, right):
    return jnp.dot(left, right.T, preferred_element_type=jnp.float32)


def swish(value):
    return value * jax.nn.sigmoid(value)


def swish_slope(value):
    sigma = jax.nn.sigmoid(value)
    return sigma * (1.0 + value * (1.0 - sigma))


def layer_norm(stream, gain):
    centred = stream - jnp.mean(stream, axis=-1, keepdims=True)
    inverse = lax.rsqrt(jnp.mean(centred * centred, axis=-1, keepdims=True) + EPS)
    unit = centred * inverse
    return ((unit * gain).astype(jnp.bfloat16), unit, inverse)


def norm_back(dnormed, unit, inverse, gain):
    scaled = dnormed * gain
    dstream = inverse * (
        scaled
        - jnp.mean(scaled, axis=-1, keepdims=True)
        - unit * jnp.mean(scaled * unit, axis=-1, keepdims=True)
    )
    return (dstream, jnp.sum(dnormed * unit, axis=0))


def position_terms(query_start, rows, keys, head_terms):
    query_pos = query_start + lax.iota(jnp.int32, rows)
    key_pos = lax.iota(jnp.int32, keys)
    offset = query_pos[:, None] - key_pos[None, :]
    distance = jnp.abs(offset).astype(jnp.float32)
    far = (offset >= RFAR).astype(jnp.float32)
    bias = far[None] * head_terms[1][:, None, None] - distance[None] * head_terms[0][:, None, None]
    return (bias, distance, far)


def split_heads(queries, keyvals):
    rows, width = queries.shape
    keys = keyvals.shape[0]
    query_heads = queries.reshape(rows, H, HD)
    key_heads = keyvals[:, :width].reshape(keys, H, HD)
    value_heads = keyvals[:, width:].reshape(keys, H, HD)
    return (query_heads, key_heads, value_heads)


def score_heads(query_heads, key_heads, bias, key_valid):
    scores = jnp.einsum("qhd,khd->hqk", query_heads, key_heads, preferred_element_type=jnp.float32)
    scores = scores * HD ** (-0.5) + bias
    return jnp.where(key_valid[None, None, :], scores, NEGATIVE)


def attend_forward(queries, keyvals, bias, key_valid):
    rows, width = queries.shape
    query_heads, key_heads, value_heads = split_heads(queries, keyvals)
    scores = score_heads(query_heads, key_heads, bias, key_valid)
    top = jnp.max(scores, axis=-1, keepdims=True)
    logsum = top + jnp.log(jnp.sum(jnp.exp(scores - top), axis=-1, keepdims=True))
    probs = jnp.exp(scores - logsum).astype(jnp.bfloat16)
    context = jnp.einsum("hqk,khd->qhd", probs, value_heads, preferred_element_type=jnp.float32)
    return (context.reshape(rows, width).astype(jnp.bfloat16), logsum)


def attend_backward(queries, keyvals, bias, distance, far, key_valid, logsum, dcontext):
    rows, width = queries.shape
    keys = keyvals.shape[0]
    query_heads, key_heads, value_heads = split_heads(queries, keyvals)
    scores = score_heads(query_heads, key_heads, bias, key_valid)
    probs = jnp.exp(scores - logsum)
    dcontext_heads = dcontext.reshape(rows, H, HD)
    dprobs = jnp.einsum(
        "qhd,khd->hqk", dcontext_heads, value_heads, preferred_element_type=jnp.float32
    )
    dscores = probs * (dprobs - jnp.sum(probs * dprobs, axis=-1, keepdims=True))
    slope_grad = -jnp.sum(dscores * distance[None], axis=(1, 2))
    far_grad = jnp.sum(dscores * far[None], axis=(1, 2))
    dscores_low = dscores.astype(jnp.bfloat16)
    probs_low = probs.astype(jnp.bfloat16)
    factor = HD ** (-0.5)
    dquery = (
        jnp.einsum("hqk,khd->qhd", dscores_low, key_heads, preferred_element_type=jnp.float32)
        * factor
    )
    dkey = (
        jnp.einsum("hqk,qhd->khd", dscores_low, query_heads, preferred_element_type=jnp.float32)
        * factor
    )
    dvalue = jnp.einsum(
        "hqk,qhd->khd", probs_low, dcontext_heads, preferred_element_type=jnp.float32
    )
    dkeyvals = jnp.concatenate([dkey.reshape(keys, width), dvalue.reshape(keys, width)], axis=1)
    return (dquery.reshape(rows, width), dkeyvals, jnp.stack([slope_grad, far_grad]))


def depthwise_apply(padded, kernel, count):
    kernel_f = kernel.astype(jnp.float32)
    padded_f = padded.astype(jnp.float32)
    total = jnp.zeros(padded.shape[:-2] + (count, padded.shape[-1]), jnp.float32)
    for tap in range(kernel.shape[1]):
        total = total + padded_f[..., tap : tap + count, :] * kernel_f[:, tap]
    return total


def depthwise_back(padded, dpadded, ddepth, kernel, count):
    kernel_f = kernel.astype(jnp.float32)
    padded_f = padded.astype(jnp.float32)
    span = kernel.shape[1] - 1
    dgated = jnp.zeros(ddepth.shape, jnp.float32)
    columns = []
    for tap in range(kernel.shape[1]):
        dgated = dgated + dpadded[..., span - tap : span - tap + count, :] * kernel_f[:, tap]
        columns.append(
            jnp.sum(
                (padded_f[..., tap : tap + count, :] * ddepth).reshape(-1, kernel.shape[0]), axis=0
            )
        )
    return (dgated, jnp.stack(columns, axis=1))


def column_blocks(stack, width):
    extra = -stack.shape[2] % width
    if extra:
        stack = jnp.pad(stack, ((0, 0), (0, 0), (0, extra)))
    return [stack[:, :, at : at + width] for at in range(0, stack.shape[2], width)]


def per_device(
    tokens,
    lengths,
    cotangent,
    first_up,
    first_down,
    project_in,
    project_out,
    pointwise_in,
    depthwise,
    pointwise_out,
    second_up,
    second_down,
    gains,
    batch_shift,
    head_terms,
):
    micro_count, seqs, local, width = tokens.shape
    rows = seqs * local
    full = local * lax.axis_size("ctx")
    half = depthwise.shape[1] // 2
    query_start = lax.axis_index("ctx") * local
    frame_pos = query_start + lax.iota(jnp.int32, local)
    key_pos = lax.iota(jnp.int32, full)
    bias, distance, far = position_terms(query_start, local, full, head_terms)
    taps = depthwise.shape[1]
    gain_count = gains.shape[0]
    small_params = lax.all_gather(
        jnp.concatenate([depthwise, gains.T, batch_shift[:, None]], axis=1),
        "fsdp",
        axis=0,
        tiled=True,
    )
    all_depthwise = small_params[:, :taps]
    all_gains = small_params[:, taps : taps + gain_count].T
    all_shift = small_params[:, taps + gain_count]
    outputs = []
    dinputs = []
    totals = None
    for micro in range(micro_count):
        front_weights = (
            lax.all_gather(first_up, "fsdp", axis=0, tiled=True),
            lax.all_gather(first_down, "fsdp", axis=0, tiled=True),
            lax.all_gather(project_in, "fsdp", axis=0, tiled=True),
            lax.all_gather(project_out, "fsdp", axis=0, tiled=True),
            lax.all_gather(pointwise_in, "fsdp", axis=0, tiled=True),
            all_depthwise,
            lax.all_gather(pointwise_out, "fsdp", axis=0, tiled=True),
            lax.all_gather(second_up, "fsdp", axis=0, tiled=True),
            lax.all_gather(second_down, "fsdp", axis=0, tiled=True),
            all_gains,
            all_shift,
        )
        (
            whole_first_up,
            whole_first_down,
            whole_project_in,
            whole_project_out,
            whole_pointwise_in,
            whole_depthwise,
            whole_pointwise_out,
            whole_second_up,
            whole_second_down,
            whole_gains,
            whole_shift,
        ) = front_weights
        gain_rows = whole_gains.astype(jnp.float32)
        shift_row = whole_shift.astype(jnp.float32)
        length_now = lengths[micro]
        mask = (frame_pos[None, :] < length_now[:, None]).astype(jnp.float32).reshape(rows, 1)
        key_valid = key_pos[None, :] < length_now[:, None]
        stream_in = tokens[micro].reshape(rows, width).astype(jnp.float32)
        normed_first, unit_first, inverse_first = layer_norm(stream_in, gain_rows[0])
        up_first = product(normed_first, whole_first_up)
        act_first = swish(up_first).astype(jnp.bfloat16)
        stream_first = stream_in + 0.5 * product(act_first, whole_first_down)
        normed_attend, unit_attend, inverse_attend = layer_norm(stream_first, gain_rows[1])
        triple = product(normed_attend, whole_project_in).astype(jnp.bfloat16)
        queries = triple[:, :width].reshape(seqs, local, width)
        keyvals = lax.all_gather(
            triple[:, width:].reshape(seqs, local, 2 * width), "ctx", axis=1, tiled=True
        )
        context, logsum = jax.vmap(attend_forward, in_axes=(0, 0, None, 0))(
            queries, keyvals, bias, key_valid
        )
        context = context.reshape(rows, width)
        stream_attend = stream_first + product(context, whole_project_out)
        normed_conv, unit_conv, inverse_conv = layer_norm(stream_attend, gain_rows[2])
        expanded = product(normed_conv, whole_pointwise_in)
        linear = expanded[:, :width]
        gate_sigma = jax.nn.sigmoid(expanded[:, width:])
        gated_low = (linear * gate_sigma * mask).astype(jnp.bfloat16).reshape(seqs, local, width)
        padded = extended(gated_low, (("ctx", 1),), half)
        depth = depthwise_apply(padded, whole_depthwise, local).reshape(rows, width)
        total, count = lax.psum((jnp.sum(mask * depth, axis=0), jnp.sum(mask)), ("fsdp", "ctx"))
        bn_mean = total / count
        centred_bn = depth - bn_mean
        spread = lax.psum(jnp.sum(mask * centred_bn * centred_bn, axis=0), ("fsdp", "ctx"))
        variance = spread / count
        inverse_bn = lax.rsqrt(variance + EPS)
        unit_bn = centred_bn * inverse_bn
        shifted = unit_bn * gain_rows[5] + shift_row
        act_conv = swish(shifted).astype(jnp.bfloat16)
        stream_conv = stream_attend + product(act_conv, whole_pointwise_out)
        normed_second, unit_second, inverse_second = layer_norm(stream_conv, gain_rows[3])
        up_second = product(normed_second, whole_second_up)
        act_second = swish(up_second).astype(jnp.bfloat16)
        stream_second = stream_conv + 0.5 * product(act_second, whole_second_down)
        out_low, unit_out, inverse_out = layer_norm(stream_second, gain_rows[4])
        outputs.append(out_low.reshape(seqs, local, width))
        back_weights = (
            lax.all_gather(first_up, "fsdp", axis=0, tiled=True),
            lax.all_gather(first_down, "fsdp", axis=0, tiled=True),
            lax.all_gather(project_in, "fsdp", axis=0, tiled=True),
            lax.all_gather(project_out, "fsdp", axis=0, tiled=True),
            lax.all_gather(pointwise_in, "fsdp", axis=0, tiled=True),
            all_depthwise,
            lax.all_gather(pointwise_out, "fsdp", axis=0, tiled=True),
            lax.all_gather(second_up, "fsdp", axis=0, tiled=True),
            lax.all_gather(second_down, "fsdp", axis=0, tiled=True),
            all_gains,
        )
        (
            back_first_up,
            back_first_down,
            back_project_in,
            back_project_out,
            back_pointwise_in,
            back_depthwise,
            back_pointwise_out,
            back_second_up,
            back_second_down,
            back_gains,
        ) = back_weights
        gain_rows = back_gains.astype(jnp.float32)
        dout = cotangent[micro].reshape(rows, width).astype(jnp.float32)
        dsecond_stream, gain_out = norm_back(dout, unit_out, inverse_out, gain_rows[4])
        dsecond_low = (0.5 * dsecond_stream).astype(jnp.bfloat16)
        dup_second = (product_right(dsecond_low, back_second_down) * swish_slope(up_second)).astype(
            jnp.bfloat16
        )
        dtemp, gain_second = norm_back(
            product_right(dup_second, back_second_up), unit_second, inverse_second, gain_rows[3]
        )
        dconv_stream = dsecond_stream + dtemp
        dconv_low = dconv_stream.astype(jnp.bfloat16)
        dshift = product_right(dconv_low, back_pointwise_out) * swish_slope(shifted)
        grad_shift = jnp.sum(dshift, axis=0)
        grad_gamma = jnp.sum(dshift * unit_bn, axis=0)
        sum_shift, sum_cross = lax.psum((grad_shift, grad_gamma), ("fsdp", "ctx"))
        ddepth = (
            inverse_bn
            * gain_rows[5]
            * (dshift - mask * sum_shift / count - mask * unit_bn * sum_cross / count)
        )
        ddepth = ddepth.reshape(seqs, local, width)
        dpadded = extended(ddepth.astype(jnp.bfloat16), (("ctx", 1),), half).astype(ddepth.dtype)
        dgated, grad_depth = depthwise_back(padded, dpadded, ddepth, back_depthwise, local)
        dgated = dgated.reshape(rows, width) * mask
        dexpanded = jnp.concatenate(
            [dgated * gate_sigma, dgated * linear * gate_sigma * (1.0 - gate_sigma)], axis=1
        ).astype(jnp.bfloat16)
        dtemp, gain_conv = norm_back(
            product_right(dexpanded, back_pointwise_in), unit_conv, inverse_conv, gain_rows[2]
        )
        dattend_stream = dconv_stream + dtemp
        dattend_low = dattend_stream.astype(jnp.bfloat16)
        dcontext = (
            product_right(dattend_low, back_project_out)
            .astype(jnp.bfloat16)
            .reshape(seqs, local, width)
        )
        dquery, dkeyvals_full, dheads = jax.vmap(
            attend_backward, in_axes=(0, 0, None, None, None, 0, 0, 0)
        )(queries, keyvals, bias, distance, far, key_valid, logsum, dcontext)
        dkeyvals = lax.psum_scatter(
            dkeyvals_full.astype(jnp.bfloat16), "ctx", scatter_dimension=1, tiled=True
        ).astype(jnp.float32)
        dtriple = (
            jnp.concatenate([dquery, dkeyvals], axis=2)
            .astype(jnp.bfloat16)
            .reshape(rows, 3 * width)
        )
        dtemp, gain_attend = norm_back(
            product_right(dtriple, back_project_in), unit_attend, inverse_attend, gain_rows[1]
        )
        dfirst_stream = dattend_stream + dtemp
        dfirst_low = (0.5 * dfirst_stream).astype(jnp.bfloat16)
        dup_first = (product_right(dfirst_low, back_first_down) * swish_slope(up_first)).astype(
            jnp.bfloat16
        )
        dtemp, gain_first = norm_back(
            product_right(dup_first, back_first_up), unit_first, inverse_first, gain_rows[0]
        )
        dinputs.append((dfirst_stream + dtemp).astype(jnp.bfloat16).reshape(seqs, local, width))
        gain_grads = jnp.stack(
            [gain_first, gain_attend, gain_conv, gain_second, gain_out, grad_gamma]
        )
        step_grads = (
            product_left(normed_first, dup_first),
            product_left(act_first, dfirst_low),
            product_left(normed_attend, dtriple),
            product_left(context, dattend_low),
            product_left(normed_conv, dexpanded),
            grad_depth,
            product_left(act_conv, dconv_low),
            product_left(normed_second, dup_second),
            product_left(act_second, dsecond_low),
            gain_grads,
            grad_shift,
            jnp.sum(dheads, axis=0),
        )
        totals = (
            step_grads
            if totals is None
            else tuple((old + new for old, new in zip(totals, step_grads)))
        )
    (
        grad_first_up,
        grad_first_down,
        grad_project_in,
        grad_project_out,
        grad_pointwise_in,
        grad_depthwise,
        grad_pointwise_out,
        grad_second_up,
        grad_second_down,
        grad_gains,
        grad_shift_all,
        grad_heads,
    ) = totals
    shards = lax.axis_size("fsdp")
    gain_count = grad_gains.shape[0]
    small = jnp.concatenate(
        [grad_depthwise, grad_gains.T, grad_shift_all[:, None]], axis=1
    )
    heads_flat = jnp.broadcast_to(grad_heads.reshape(1, 1, -1), (shards, 1, grad_heads.size))
    weight_grads = (
        grad_first_up,
        grad_first_down,
        grad_project_in,
        grad_project_out,
        grad_pointwise_in,
        grad_pointwise_out,
        grad_second_up,
        grad_second_down,
        small,
    )
    pieces = []
    for grad in weight_grads:
        pieces.extend(column_blocks(grad.astype(jnp.bfloat16).reshape(shards, -1, grad.shape[1]), width))
    pieces.extend(column_blocks(heads_flat.astype(jnp.bfloat16), width))
    packed = jnp.concatenate(pieces, axis=1)
    shard = lax.psum_scatter(packed, "fsdp", scatter_dimension=0, tiled=True)
    summed_pack = lax.psum(shard[0], "ctx").astype(jnp.float32)
    start = 0
    unpacked = []
    for grad in weight_grads:
        rows_here = grad.shape[0] // shards
        blocks = []
        for column in range(0, grad.shape[1], width):
            blocks.append(summed_pack[start : start + rows_here])
            start += rows_here
        unpacked.append(jnp.concatenate(blocks, axis=1)[:, : grad.shape[1]])
    heads_row = summed_pack[start, : grad_heads.size].reshape(grad_heads.shape)
    taps = depthwise.shape[1]
    small_sum = unpacked[8]
    summed = (
        unpacked[0],
        unpacked[1],
        unpacked[2],
        unpacked[3],
        unpacked[4],
        small_sum[:, :taps],
        unpacked[5],
        unpacked[6],
        unpacked[7],
        small_sum[:, taps : taps + gain_count].T,
        small_sum[:, taps + gain_count],
        heads_row[None],
    )
    return (
        jnp.stack(outputs),
        jnp.stack(dinputs),
        summed[0],
        summed[1],
        summed[2],
        summed[3],
        summed[4],
        summed[5],
        summed[6],
        summed[7],
        summed[8],
        summed[9],
        summed[10],
        summed[11][0],
    )


def solution(mesh):
    in_specs = (
        P(None, "fsdp", "ctx", None),
        P(None, "fsdp"),
        P(None, "fsdp", "ctx", None),
        P("fsdp", None),
        P("fsdp", None),
        P("fsdp", None),
        P("fsdp", None),
        P("fsdp", None),
        P("fsdp", None),
        P("fsdp", None),
        P("fsdp", None),
        P("fsdp", None),
        P(None, "fsdp"),
        P("fsdp"),
        P(),
    )
    out_specs = (
        P(None, "fsdp", "ctx", None),
        P(None, "fsdp", "ctx", None),
        P("fsdp", None),
        P("fsdp", None),
        P("fsdp", None),
        P("fsdp", None),
        P("fsdp", None),
        P("fsdp", None),
        P("fsdp", None),
        P("fsdp", None),
        P("fsdp", None),
        P(None, "fsdp"),
        P("fsdp"),
        P(),
    )
    return jax.shard_map(
        per_device, mesh=mesh, in_specs=in_specs, out_specs=out_specs, check_vma=False
    )
```

profile of v0, /device:TPU:0, one launch (start us, length us, event | category | flops | bytes accessed | tf_op | source)
XLA Modules:
  0.0 1014.8 jit_solution(4822305680818637366)
XLA Ops:
  10.2 32.4 %all-gather.2 = bf16[8,64,38]{1,2,0:T(8,128)(2,1)S(1)} all-gather(bf16[1,64,38]{1,2,0:T(8,128)(2,1)S(1)} %maximum_bitcast_fusion), channel_id=1, replica_groups=mesh['fsdp'=8,'ctx'=4] {'fsdp'}, dimensions={0}, use_global_device_ids=true | all-gather | bytes 43776 | tf_op jit(solution)/shard_map/all_gather | solution.py:192
  45.7 16.5 %all-gather.12.cloned.1.call-done = bf16[512,2048]{1,0:T(8,128)(2,1)} async-done(((bf16[64,2048]{1,0:T(8,128)(2,1)}), bf16[512,2048]{1,0:T(8,128)(2,1)}) %all-gather.12.cloned.1.call-update) | async-done | bytes 2097168 | tf_op jit(solution)/shard_map/all_gather | solution.py:206
  64.4 47.6 %all-gather.14.cloned.1.call-done = bf16[2048,512]{1,0:T(8,128)(2,1)} async-done(((bf16[256,512]{1,0:T(8,128)(2,1)}), bf16[2048,512]{1,0:T(8,128)(2,1)}) %all-gather.14.cloned.1.call-update) | async-done | bytes 2097168 | tf_op jit(solution)/shard_map/all_gather | solution.py:207
  114.4 42.5 %all-gather.16.cloned.1.call-done = bf16[512,1536]{1,0:T(8,128)(2,1)} async-done(((bf16[64,1536]{1,0:T(8,128)(2,1)}), bf16[512,1536]{1,0:T(8,128)(2,1)}) %all-gather.16.cloned.1.call-update) | async-done | bytes 1572880 | tf_op jit(solution)/shard_map/all_gather | solution.py:208
  176.3 31.4 %all_gather.27 = bf16[512,512]{1,0:T(8,128)(2,1)S(1)} all-gather(bf16[64,512]{1,0:T(8,128)(2,1)S(1)} %copy-done.125), channel_id=1, replica_groups=mesh['fsdp'=8,'ctx'=4] {'fsdp'}, dimensions={0}, use_global_device_ids=true | all-gather | bytes 589824 | tf_op jit(solution)/shard_map/all_gather | solution.py:209
  207.6 34.2 %all_gather.29 = bf16[512,512]{1,0:T(8,128)(2,1)} all-gather(bf16[64,512]{1,0:T(8,128)(2,1)S(1)} %copy-done.126), channel_id=1, replica_groups=mesh['fsdp'=8,'ctx'=4] {'fsdp'}, dimensions={0}, use_global_device_ids=true | all-gather | bytes 589824 | tf_op jit(solution)/shard_map/all_gather | solution.py:212
  264.2 4.7 collective-permute-start.2
  277.7 40.1 %all-reduce.4 = (f32[512]{0:T(512)}, f32[]{:T(128)}, f32[512]{0:T(512)}, f32[]{:T(128)}) all-reduce(f32[512]{0:T(512)} %get-tuple-element.194, f32[]{:T(128)} %get-tuple-element.192, f32[512]{0:T(512)} %get-tuple-element.190, f32[]{:T(128)} %get-tuple-element.188), channel_id=1, replica_groups=mesh['fsdp'=8,'ctx'=4] {'fsdp','ctx'}, use_global_device_ids=true, to_apply=%region_27.28 | all-reduce | flops 1026 | bytes 8208 | tf_op jit(solution)/shard_map/psum | solution.py:259
  324.8 42.3 %all-reduce.3 = (f32[512]{0:T(512)}, f32[512]{0:T(512)}) all-reduce(f32[512]{0:T(512)} %fusion.75, f32[512]{0:T(512)} %fusion.74), channel_id=1, replica_groups=mesh['fsdp'=8,'ctx'=4] {'fsdp','ctx'}, use_global_device_ids=true, to_apply=%region_31.32 | all-reduce | flops 1024 | bytes 8192 | tf_op jit(solution)/shard_map/psum | solution.py:262
  375.2 3.2 fusion.268
  395.6 50.5 %all-reduce.2 = (f32[512]{0:T(512)}, f32[512]{0:T(512)}, f32[512]{0:T(512)}, f32[512]{0:T(512)}) all-reduce(f32[512]{0:T(512)} %get-tuple-element.161, f32[512]{0:T(512)} %copy-done.271, f32[512]{0:T(512)} %get-tuple-element.159, f32[512]{0:T(512)} %copy-done.272), channel_id=1, replica_groups=mesh['fsdp'=8,'ctx'=4] {'fsdp','ctx'}, use_global_device_ids=true, to_apply=%region_59.60 | all-reduce | flops 2048 | bytes 16384 | tf_op jit(solution)/shard_map/psum | solution.py:314
  456.2 3.5 fusion.236
  530.0 5.6 collective-permute-start.6
  537.0 4.7 add_convert_fusion
  545.4 4.0 copy.133
  575.1 6.0 copy.144
  598.3 5.5 stack.319
  603.8 5.5 stack.287
  613.8 4.7 copy.142
  640.2 7.2 reduce-scatter.10.cloned.1.call-done
  649.1 3.5 fusion.213
  697.0 24.8 %concatenate.154 = bf16[8,1537,512]{1,2,0:T(8,128)(2,1)} concatenate(bf16[8,64,512]{1,2,0:T(8,128)(2,1)} %copy.148, bf16[8,64,512]{1,2,0:T(8,128)(2,1)} %copy.149, bf16[8,64,512]{1,2,0:T(8,128)(2,1)} %copy.150, bf16[8,64,512]{1,2,0:T(8,128)(2,1)} %copy.151, bf16[8,256,512]{1,2,0:T(8,128)(2,1)} %copy.130, bf16[8,64,512]{1,2,0:T(8,128)(2,1)} %copy.152, bf16[8,64,512]{1,2,0:T(8,128)(2,1)} %copy.153, ...), dimensions={1} | concatenate | bytes 25182208 | tf_op jit(solution)/shard_map/concatenate | solution.py:417
  723.6 220.5 %reduce-scatter.8.cloned.1.call-done = bf16[1,1537,512]{1,2,0:T(8,128)(2,1)} async-done(((bf16[8,1537,512]{1,2,0:T(8,128)(2,1)}), bf16[1,1537,512]{1,2,0:T(8,128)(2,1)}) %reduce-scatter.8.cloned.1.call-update) | async-done | bytes 1573904 | tf_op jit(solution)/shard_map/reduce_scatter | solution.py:418
  945.2 45.3 %all-reduce.7.cloned.1.call-done = bf16[1537,512]{0,1:T(8,128)(2,1)} async-done(((bf16[1537,512]{0,1:T(8,128)(2,1)}), bf16[1537,512]{0,1:T(8,128)(2,1)}) %all-reduce.7.cloned.1.call-update) | async-done | bytes 1573904 | tf_op jit(solution)/shard_map/psum | solution.py:419
  (989 shorter events, 310.0 us)
Async XLA Ops:
  7.2 55.0 %all-gather.12.cloned.1.call-start = ((), (), s32[]{:S(2)}) async-start(), calls=%async_computation.3 | async-start | bytes 2359296 | tf_op jit(solution)/shard_map/all_gather | solution.py:206
  7.9 104.1 %all-gather.14.cloned.1.call-start = ((), (), s32[]{:S(2)}) async-start(), calls=%async_computation.4 | async-start | bytes 2359296 | tf_op jit(solution)/shard_map/all_gather | solution.py:207
  8.7 148.3 %all-gather.16.cloned.1.call-start = ((), (), s32[]{:S(2)}) async-start(), calls=%async_computation.5 | async-start | bytes 1769472 | tf_op jit(solution)/shard_map/all_gather | solution.py:208
  9.4 233.4 %all-gather.26.cloned.1.call-start = ((), (), s32[]{:S(2)}) async-start(), calls=%async_computation.12 | async-start | bytes 1310720 | tf_op jit(solution)/shard_map/all_gather | solution.py:244
  159.6 86.5 %all-gather.24.cloned.1.call-start = ((), (), s32[]{:S(2)}) async-start(), calls=%async_computation.11 | async-start | bytes 1310720 | tf_op jit(solution)/shard_map/all_gather | solution.py:244
  164.2 89.4 %all-gather.18.cloned.1.call-start = ((), (), s32[]{:S(2)}) async-start(), calls=%async_computation.6 | async-start | bytes 1179648 | tf_op jit(solution)/shard_map/all_gather | solution.py:210
  164.8 210.4 %all-gather.20.cloned.1.call-start = ((), (), s32[]{:S(2)}) async-start(), calls=%async_computation.7 | async-start | bytes 2359296 | tf_op jit(solution)/shard_map/all_gather | solution.py:213
  165.6 212.8 %all-gather.22.cloned.1.call-start = ((), (), s32[]{:S(2)}) async-start(), calls=%async_computation.8 | async-start | bytes 2359296 | tf_op jit(solution)/shard_map/all_gather | solution.py:214
  166.3 471.7 %reduce-scatter.12.cloned.1.call-start = ((), (), s32[]{:S(2)}) async-start(), calls=%async_computation.14 | async-start | bytes 1310720
  256.1 14.5 %collective-permute-start = (bf16[1,15,512]{2,1,0:T(8,128)(2,1)S(1)}, bf16[1,15,512]{2,1,0:T(8,128)(2,1)S(1)}, u32[]{:S(2)}, u32[]{:S(2)}) collective-permute-start(bf16[1,15,512]{2,1,0:T(8,128)(2,1)S(1)} %get-tuple-element.240), channel_id=1, source_target_pairs={{0,1},{1,2},{2,3},{4,5},{5,6},{6,7},{8,9},{9,10},{10,11},{12,13},{... | collective-permute-start | bytes 46088 | tf_op jit(solution)/shard_map/ppermute | solution.py:20
  257.4 13.3 %collective-permute-start.1 = (bf16[1,15,512]{2,1,0:T(8,128)(2,1)S(1)}, bf16[1,15,512]{2,1,0:T(8,128)(2,1)S(1)}, u32[]{:S(2)}, u32[]{:S(2)}) collective-permute-start(bf16[1,15,512]{2,1,0:T(8,128)(2,1)S(1)} %get-tuple-element.241), channel_id=1, source_target_pairs={{1,0},{2,1},{3,2},{5,4},{6,5},{7,6},{9,8},{10,9},{11,10},{13,12},{... | collective-permute-start | bytes 46088 | tf_op jit(solution)/shard_map/ppermute | solution.py:23
  264.2 6.5 collective-permute-start.2
  269.0 4.3 collective-permute-start.3
  525.5 26.8 %collective-permute-start.4 = (bf16[1,15,512]{2,1,0:T(8,128)(2,1)}, bf16[1,15,512]{2,1,0:T(8,128)(2,1)}, u32[]{:S(2)}, u32[]{:S(2)}) collective-permute-start(bf16[1,15,512]{2,1,0:T(8,128)(2,1)} %get-tuple-element.236), channel_id=1, source_target_pairs={{0,1},{1,2},{2,3},{4,5},{5,6},{6,7},{8,9},{9,10},{10,11},{12,13},{... | collective-permute-start | bytes 46088 | tf_op jit(solution)/shard_map/ppermute | solution.py:20
  527.4 25.0 %collective-permute-start.5 = (bf16[1,15,512]{2,1,0:T(8,128)(2,1)}, bf16[1,15,512]{2,1,0:T(8,128)(2,1)}, u32[]{:S(2)}, u32[]{:S(2)}) collective-permute-start(bf16[1,15,512]{2,1,0:T(8,128)(2,1)} %get-tuple-element.237), channel_id=1, source_target_pairs={{1,0},{2,1},{3,2},{5,4},{6,5},{7,6},{9,8},{10,9},{11,10},{13,12},{... | collective-permute-start | bytes 46088 | tf_op jit(solution)/shard_map/ppermute | solution.py:23
  530.0 19.3 %collective-permute-start.6 = (bf16[1,15,512]{2,1,0:T(8,128)(2,1)}, bf16[1,15,512]{2,1,0:T(8,128)(2,1)}, u32[]{:S(2)}, u32[]{:S(2)}) collective-permute-start(bf16[1,15,512]{2,1,0:T(8,128)(2,1)} %get-tuple-element.238), channel_id=1, source_target_pairs={{0,1},{1,2},{2,3},{4,5},{5,6},{6,7},{8,9},{9,10},{10,11},{12,13},{... | collective-permute-start | bytes 46088 | tf_op jit(solution)/shard_map/ppermute | solution.py:20
  535.6 13.7 %collective-permute-start.7 = (bf16[1,15,512]{2,1,0:T(8,128)(2,1)}, bf16[1,15,512]{2,1,0:T(8,128)(2,1)}, u32[]{:S(2)}, u32[]{:S(2)}) collective-permute-start(bf16[1,15,512]{2,1,0:T(8,128)(2,1)} %get-tuple-element.239), channel_id=1, source_target_pairs={{1,0},{2,1},{3,2},{5,4},{6,5},{7,6},{9,8},{10,9},{11,10},{13,12},{... | collective-permute-start | bytes 46088 | tf_op jit(solution)/shard_map/ppermute | solution.py:23
  584.1 63.3 %reduce-scatter.10.cloned.1.call-start = ((), (), s32[]{:S(2)}) async-start(), calls=%async_computation.13 | async-start | bytes 1310720
  620.2 323.9 %reduce-scatter.8.cloned.1.call-start = ((), (), s32[]{:S(2)}) async-start(), calls=%async_computation.9 | async-start | bytes 15335424 | tf_op jit(solution)/shard_map/reduce_scatter | solution.py:418
  722.0 222.2 %copy-start.72 = (f32[128,512]{1,0:T(8,128)S(1)}, f32[128,512]{1,0:T(8,128)}, u32[]{:S(2)}) copy-start(f32[128,512]{1,0:T(8,128)} %copy-done.71) | copy-start | bytes 786436
  722.0 222.2 %copy-start.74 = (f32[128,512]{1,0:T(8,128)S(1)}, f32[128,512]{1,0:T(8,128)}, u32[]{:S(2)}) copy-start(f32[128,512]{1,0:T(8,128)} %copy-done.73) | copy-start | bytes 786436
  722.0 222.2 %copy-start.99 = (f32[128,512]{1,0:T(8,128)S(1)}, f32[128,512]{1,0:T(8,128)}, u32[]{:S(2)}) copy-start(f32[128,512]{1,0:T(8,128)} %copy-done.98) | copy-start | bytes 786436
  722.0 222.2 %copy-start.115 = (f32[128,512]{1,0:T(8,128)S(1)}, f32[128,512]{1,0:T(8,128)}, u32[]{:S(2)}) copy-start(f32[128,512]{1,0:T(8,128)} %get-tuple-element.323) | copy-start | bytes 786436
  722.0 268.4 %all-reduce.7.cloned.1.call-start = ((), (), s32[]{:S(2)}) async-start(), calls=%async_computation.10 | async-start | bytes 3407872 | tf_op jit(solution)/shard_map/psum | solution.py:419
  (318 other events, 4354.7 us)
Sparse Core Ops, SparseCore 0:
  10.1 52.0 all-gather.11
  64.3 47.6 all-gather.13
  114.2 42.7 all-gather.15
  159.7 15.0 all-gather.25
  176.8 16.6 all-gather.23
  195.5 42.6 all-gather.17
  240.3 48.0 all-gather.19
  290.6 48.0 all-gather.21
  584.2 26.9 reduce-scatter.11
  620.4 26.9 reduce-scatter.9
  722.1 222.0 reduce-scatter.7
  946.3 44.0 all-reduce.6
where the time goes:
time: 1030 us; the launch traced here: 1010 us
  waiting for transfers between devices  386 us (37%)
  blocking collectives  231 us (22%)
  local copies, waits for them, and re-layouts  207 us (20%)
  matrix products  91 us (9%)
  other arithmetic  61 us (6%)
  starting transfers between devices  20 us (2%)
  between operations  18.6 us (2%)
    reduce_scatter x1, waiting for transfers between devices, per_device(): shard = lax.psum_scatter(packed, 'fsdp', scatter_dimension=0, tiled=True)  221 us
    another operation x64, local copies, waits for them, and re-layouts, depthwise_back(): return (dgated, jnp.stack(columns, axis=1))  74.1 us
    unnamed x672, local copies, waits for them, and re-layouts  67.3 us
    psum x1, blocking collectives, per_device(): sum_shift, sum_cross = lax.psum((grad_shift, grad_gamma), ('fsdp', 'ctx'))  50.5 us
    all_gather x1, waiting for transfers between devices, per_device(): lax.all_gather(first_down, 'fsdp', axis=0, tiled=True)  47.6 us
    psum x1, waiting for transfers between devices, per_device(): summed_pack = lax.psum(shard[0], 'ctx').astype(jnp.float32)  45.3 us
    all_gather x1, waiting for transfers between devices, per_device(): lax.all_gather(project_in, 'fsdp', axis=0, tiled=True)  42.5 us
    psum x1, blocking collectives, per_device(): lax.psum(jnp.sum(mask * centred_bn * centred_bn, axis=0), ('fsdp', 'ctx'))  42.3 us
  transfers between devices with their start and end apart: 20, of which 7 were waited for; matrix products, arithmetic and copies ran while one was open for 13% of the time, Pallas kernels for 0%

commit v1 on v0

v1 whole, which is shorter than its diff:
```python
import functools

import jax
import jax.numpy as jnp
from jax import lax
from jax.experimental import pallas as pl
from jax.experimental.pallas import tpu as pltpu
from jax.sharding import PartitionSpec as P

H = 8
HD = 64
RFAR = 256
HALO = 16
VMEM_LIMIT = 60 * 1024 * 1024


EPS = 1e-05
NEGATIVE = -1e30
MESH = pl.DeviceIdType.MESH
ANY = pl.BlockSpec(memory_space=pl.ANY)
VMEM = pl.BlockSpec(memory_space=pltpu.VMEM)
SMEM = pl.BlockSpec(memory_space=pltpu.SMEM)


def rotated(index, step, count):
    return lax.rem(index + step + count, count)


def other_of(index):
    return index + 1 - 2 * lax.rem(index, 2)


def greet(peers):
    barrier = pltpu.get_barrier_semaphore()
    for peer in peers:
        pl.semaphore_signal(barrier, inc=1, device_id=peer, device_id_type=MESH)
    pl.semaphore_wait(barrier, len(peers))


def send(src, dst, send_sem, recv_sem, to):
    return pltpu.make_async_remote_copy(
        src_ref=src,
        dst_ref=dst,
        send_sem=send_sem,
        recv_sem=recv_sem,
        device_id=to,
        device_id_type=MESH,
    )


def gather_kernel(count, size, axis, pair, *refs):
    ins, outs = refs[:count], refs[count : 2 * count]
    keep, zs, zr, ys, yr, cs, cr = refs[2 * count :]
    me = lax.axis_index(axis)
    highs = size // 2
    low, high = lax.rem(me, 2), lax.div(me, 2)
    partner = other_of(me)

    def part(ref, mine=True):
        if pair is None:
            return ref
        width = ref.shape[-1] // 2
        side = lax.rem(lax.axis_index(pair), 2)
        start = pl.multiple_of((side if mine else 1 - side) * width, width)
        return ref.at[:, pl.ds(start, width)]

    peers = [{axis: 2 * rotated(high, d, highs) + low} for d in range(1, highs)]
    peers.append({axis: partner})
    if pair is not None:
        pair_to = {pair: other_of(lax.axis_index(pair))}
        peers.append(pair_to)
    greet(peers)

    def origin(d):
        return 2 * rotated(high, -d, highs)

    def along(a, d, landed=False):
        place = origin(d) + low if landed else me
        return send(
            part(ins[a]),
            part(outs[a].at[place]),
            zs.at[a, d],
            zr.at[a, d],
            {axis: 2 * rotated(high, d, highs) + low},
        )

    def across_first(a, landed=False):
        place = partner if landed else me
        return send(part(ins[a]), part(outs[a].at[place]), ys.at[a, 0], yr.at[a, 0], {axis: partner})

    def across(a, d, landed=False):
        place = origin(d) + (1 - low if landed else low)
        return send(
            part(outs[a].at[origin(d) + low]),
            part(outs[a].at[place]),
            ys.at[a, d],
            yr.at[a, d],
            {axis: partner},
        )

    def hand(a, place, landed=False):
        return send(
            part(outs[a].at[place]),
            part(outs[a].at[place], not landed),
            cs.at[a, place],
            cr.at[a, place],
            pair_to,
        )

    def steps(first, last, body):
        def step(i, carry):
            body(i)
            return carry

        lax.fori_loop(first, last, step, 0)

    def local(a):
        return pltpu.make_async_copy(ins[a], outs[a].at[me], keep.at[a])

    for a in range(count):
        steps(1, highs, lambda d: along(a, d).start())
        across_first(a).start()
    for a in range(count):
        local(a).start()

    def second(a):
        across_first(a, True).wait_recv()
        if pair is not None:
            hand(a, partner).start()

        def one(d):
            across(a, d, True).wait_recv()
            if pair is not None:
                hand(a, origin(d) + 1 - low).start()

        steps(1, highs, one)

    for a in range(count):

        def one(d):
            along(a, d, True).wait_recv()
            across(a, d).start()
            if pair is not None:
                hand(a, origin(d) + low).start()

        steps(1, highs, one)
        if a > 0:
            second(a - 1)
    second(count - 1)
    for a in range(count):
        if pair is not None:
            steps(1, size, lambda i: hand(a, rotated(me, i, size), True).wait_recv())
            steps(1, size, lambda i: hand(a, rotated(me, i, size)).wait_send())
        steps(1, highs, lambda d: along(a, d).wait_send())
        across_first(a).wait_send()
        steps(1, highs, lambda d: across(a, d).wait_send())
        local(a).wait()


def gather(arrays, axis, pair, ident):
    count, size = len(arrays), lax.axis_size(axis)
    highs = size // 2
    dma = pltpu.SemaphoreType.DMA
    return pl.pallas_call(
        functools.partial(gather_kernel, count, size, axis, pair),
        out_shape=[jax.ShapeDtypeStruct((size,) + a.shape, a.dtype) for a in arrays],
        in_specs=[VMEM] * count,
        out_specs=[ANY] * count,
        scratch_shapes=[
            dma((count,)),
            dma((count, highs)),
            dma((count, highs)),
            dma((count, highs)),
            dma((count, highs)),
            dma((count, size)),
            dma((count, size)),
        ],
        compiler_params=pltpu.CompilerParams(
            collective_id=ident, has_side_effects=True, vmem_limit_bytes=VMEM_LIMIT
        ),
        name="gather_" + axis,
    )(*arrays)


def scatter_kernel(count, size, axis, pair, pair_size, *refs):
    ins, outs = refs[:count], refs[count : 2 * count]
    scratch = refs[2 * count :]
    if pair is None:
        halves = ins
        rest = scratch
    else:
        halves = scratch[:count]
        rest = scratch[count:]
    lows, highs_in = rest[:count], rest[count : 2 * count]
    rest = rest[2 * count :]
    if pair is not None:
        cross = rest[:count]
        rest = rest[count:]
        cs, cr, xs, xr, fs, fr = rest[:6]
        rest = rest[6:]
    ys, yr, zs, zr = rest
    me = lax.axis_index(axis)
    highs = size // 2
    low, high = lax.rem(me, 2), lax.div(me, 2)
    partner = {axis: other_of(me)}
    peers = [{axis: 2 * rotated(high, d, highs) + low} for d in range(1, highs)]
    peers.append(partner)
    if pair is not None:
        spot = lax.axis_index(pair)
        side, place = lax.rem(spot, 2), lax.div(spot, 2)
        places = pair_size // 2
        pair_to = {pair: other_of(spot)}
        peers.append(pair_to)
        for e in range(1, places):
            peers.append({pair: 2 * rotated(place, e, places) + side})
    greet(peers)

    def columns(a, mine):
        width = halves[a].shape[-1]
        return pl.ds(pl.multiple_of((side if mine else 1 - side) * width, width), width)

    def first(a):
        return send(ins[a].at[:, :, :, columns(a, False)], halves[a], cs.at[a], cr.at[a], pair_to)

    def across(a):
        return send(halves[a].at[:, 1 - low], lows[a], ys.at[a], yr.at[a], partner)

    def along(a, d):
        to = rotated(high, d, highs)
        return send(
            lows[a].at[to],
            highs_in[a].at[d - 1],
            zs.at[a, d - 1],
            zr.at[a, d - 1],
            {axis: 2 * to + low},
        )

    def over(a, e, landed=False):
        slot = rotated(place, -e, places) if landed else place
        return send(
            cross[a].at[place],
            cross[a].at[slot],
            xs.at[a, e - 1],
            xr.at[a, e - 1],
            {pair: 2 * rotated(place, e, places) + side},
        )

    def final(a, landed=False):
        return send(
            outs[a].at[:, columns(a, True)],
            outs[a].at[:, columns(a, not landed)],
            fs.at[a],
            fr.at[a],
            pair_to,
        )

    def steps(first_step, last, body):
        def step(i, carry):
            body(i)
            return carry

        lax.fori_loop(first_step, last, step, 0)

    def stage_first(a):
        first(a).wait_recv()

        def one(i):
            for j in range(2):
                own = ins[a][i, j, :, columns(a, True)].astype(jnp.float32)
                halves[a][i, j] = (own + halves[a][i, j].astype(jnp.float32)).astype(jnp.bfloat16)

        steps(0, highs, one)
        across(a).start()

    def stage_across(a):
        across(a).wait_recv()

        def one(i):
            own = halves[a][i, low].astype(jnp.float32)
            lows[a][i] = (own + lows[a][i].astype(jnp.float32)).astype(jnp.bfloat16)

        steps(0, highs, one)
        steps(1, highs, lambda d: along(a, d).start())

    def stage_along(a):
        steps(1, highs, lambda d: along(a, d).wait_recv())

        def added(d, total):
            return total + highs_in[a][d - 1].astype(jnp.float32)

        total = lax.fori_loop(1, highs, added, lows[a][high].astype(jnp.float32))
        if pair is None:
            outs[a][...] = total.astype(outs[a].dtype)
            return
        cross[a][place] = total.astype(jnp.bfloat16)
        for e in range(1, places):
            over(a, e).start()

    def stage_over(a):
        for e in range(1, places):
            over(a, e, True).wait_recv()
        total = cross[a][0].astype(jnp.float32)
        for i in range(1, places):
            total = total + cross[a][i].astype(jnp.float32)
        outs[a][:, columns(a, True)] = total
        final(a).start()

    if pair is None:
        stages = [stage_across, stage_along]
        for a in range(count):
            across(a).start()
    else:
        stages = [stage_first, stage_across, stage_along, stage_over]
        for a in range(count):
            first(a).start()
    for step in range(count + len(stages) - 1):
        for index, stage in enumerate(stages):
            if 0 <= step - index < count:
                stage(step - index)
    for a in range(count):
        across(a).wait_send()
        steps(1, highs, lambda d: along(a, d).wait_send())
        if pair is not None:
            first(a).wait_send()
            for e in range(1, places):
                over(a, e).wait_send()
            final(a, True).wait_recv()
            final(a).wait_send()


def scatter(arrays, axis, pair, dtype, ident):
    count, size = len(arrays), lax.axis_size(axis)
    highs = size // 2
    dma = pltpu.SemaphoreType.DMA
    low_type = jnp.bfloat16
    pair_size = 2 if pair is None else lax.axis_size(pair)
    split = 1 if pair is None else 2
    tail = [(a.shape[2], a.shape[3] // split) for a in arrays]
    scratch = []
    if pair is not None:
        scratch += [pltpu.VMEM((highs, 2) + t, low_type) for t in tail]
    scratch += [pltpu.VMEM((highs,) + t, low_type) for t in tail]
    scratch += [pltpu.VMEM((highs - 1,) + t, low_type) for t in tail]
    if pair is not None:
        scratch += [pltpu.VMEM((pair_size // 2,) + t, low_type) for t in tail]
        others = (count, pair_size // 2)
        scratch += [dma((count,)), dma((count,)), dma(others), dma(others)]
        scratch += [dma((count,)), dma((count,))]
    scratch += [dma((count,)), dma((count,)), dma((count, highs)), dma((count, highs))]
    return pl.pallas_call(
        functools.partial(scatter_kernel, count, size, axis, pair, pair_size),
        out_shape=[jax.ShapeDtypeStruct(a.shape[2:], dtype) for a in arrays],
        in_specs=[VMEM] * count,
        out_specs=[VMEM] * count,
        scratch_shapes=scratch,
        compiler_params=pltpu.CompilerParams(
            collective_id=ident, has_side_effects=True, vmem_limit_bytes=VMEM_LIMIT
        ),
        name="scatter_" + axis,
    )(*arrays)


def merge_sums(parts):
    total = parts[0]
    for part in parts[1:]:
        total = total + part
    return total


def merge_moments(micro, parts):
    total = merge_sums(parts)
    sums, squares, counts = (slice(i * micro, (i + 1) * micro) for i in range(3))
    mean = total[sums] / jnp.maximum(total[counts], 1.0)
    spread = total[squares]
    for part in parts:
        shift = part[sums] / jnp.maximum(part[counts], 1.0) - mean
        spread = spread + part[counts] * shift * shift
    return jnp.concatenate([total[sums], spread, total[counts], total[3 * micro :]], axis=0)


def channel_kernel(merge, sizes, axes, in_ref, out_ref, *refs):
    slots, sums = refs[:2], refs[2]
    sems = refs[3:]
    peers = []
    for axis, size in zip(axes, sizes):
        for d in range(1, size):
            peers.append({axis: rotated(lax.axis_index(axis), d, size)})
    greet(peers)
    source = in_ref
    for stage, (axis, size) in enumerate(zip(axes, sizes)):
        me = lax.axis_index(axis)
        slot, ss, rs = slots[stage], sems[2 * stage], sems[2 * stage + 1]

        def copy(d, landed=False):
            place = rotated(me, -d, size) if landed else me
            return send(
                source, slot.at[place], ss.at[d], rs.at[d], {axis: rotated(me, d, size)}
            )

        for d in range(1, size):
            copy(d).start()
        slot[me] = source[...]
        for d in range(1, size):
            copy(d, True).wait_recv()
        total = merge([slot[i] for i in range(size)])
        for d in range(1, size):
            copy(d).wait_send()
        target = sums if stage == 0 else out_ref
        target[...] = total
        source = sums


def channel_merge(rows, merge, ident):
    axes = ("ctx", "fsdp")
    sizes = tuple(lax.axis_size(axis) for axis in axes)
    dma = pltpu.SemaphoreType.DMA
    scratch = [pltpu.VMEM((size,) + rows.shape, rows.dtype) for size in sizes]
    scratch.append(pltpu.VMEM(rows.shape, rows.dtype))
    for size in sizes:
        scratch += [dma((size,)), dma((size,))]
    return pl.pallas_call(
        functools.partial(channel_kernel, merge, sizes, axes),
        out_shape=jax.ShapeDtypeStruct(rows.shape, rows.dtype),
        in_specs=[VMEM],
        out_specs=VMEM,
        scratch_shapes=scratch,
        compiler_params=pltpu.CompilerParams(collective_id=ident, has_side_effects=True),
        name="channel_merge_" + str(ident),
    )(rows)


def positions(start, rows, keys):
    query = start + lax.broadcasted_iota(jnp.int32, (rows, keys), 0)
    key = lax.broadcasted_iota(jnp.int32, (rows, keys), 1)
    offset = query - key
    distance = jnp.abs(offset).astype(jnp.float32)
    far = (offset >= RFAR).astype(jnp.float32)
    return distance, far, key


def head_probs(query, keys, terms_ref, head, distance, far, valid):
    scores = lax.dot_general(
        query, keys, (((1,), (1,)), ((), ())), preferred_element_type=jnp.float32
    )
    bias = far * terms_ref[1, head] - distance * terms_ref[0, head]
    scores = jnp.where(valid, scores * HD ** (-0.5) + bias, NEGATIVE)
    top = jnp.max(scores, axis=-1, keepdims=True)
    raised = jnp.exp(scores - top)
    return raised / jnp.sum(raised, axis=-1, keepdims=True)


def attend_kernel(start_ref, lengths_ref, terms_ref, q_ref, kv_ref, out_ref):
    rows, width = q_ref.shape[1:]
    keys = kv_ref.shape[0] * kv_ref.shape[2]
    distance, far, key = positions(start_ref[0], rows, keys)
    valid = key < lengths_ref[pl.program_id(0)]
    for head in range(H):
        cols = slice(head * HD, (head + 1) * HD)
        key_head = kv_ref[:, 0, :, cols].reshape(keys, HD)
        value_head = kv_ref[:, 0, :, width + head * HD : width + (head + 1) * HD].reshape(keys, HD)
        probs = head_probs(q_ref[0, :, cols], key_head, terms_ref, head, distance, far, valid)
        context = jnp.dot(
            probs.astype(jnp.bfloat16), value_head, preferred_element_type=jnp.float32
        )
        out_ref[0, :, cols] = context.astype(jnp.bfloat16)


def attend_back_kernel(
    start_ref, lengths_ref, terms_ref, q_ref, kv_ref, dctx_ref, dq_ref, dkv_ref, heads_ref
):
    rows, width = q_ref.shape[1:]
    shards, _, local, _ = kv_ref.shape
    keys = shards * local
    distance, far, key = positions(start_ref[0], rows, keys)
    valid = key < lengths_ref[pl.program_id(0)]
    factor = HD ** (-0.5)
    for head in range(H):
        cols = slice(head * HD, (head + 1) * HD)
        value_cols = slice(width + head * HD, width + (head + 1) * HD)
        query = q_ref[0, :, cols]
        key_head = kv_ref[:, 0, :, cols].reshape(keys, HD)
        value_head = kv_ref[:, 0, :, value_cols].reshape(keys, HD)
        dcontext = dctx_ref[0, :, cols]
        probs = head_probs(query, key_head, terms_ref, head, distance, far, valid)
        dprobs = lax.dot_general(
            dcontext, value_head, (((1,), (1,)), ((), ())), preferred_element_type=jnp.float32
        )
        dscores = probs * (dprobs - jnp.sum(probs * dprobs, axis=-1, keepdims=True))
        heads_ref[0, head : head + 1, :] = -jnp.sum(dscores * distance, axis=0, keepdims=True)
        heads_ref[0, H + head : H + head + 1, :] = jnp.sum(dscores * far, axis=0, keepdims=True)
        low = dscores.astype(jnp.bfloat16)
        dquery = jnp.dot(low, key_head, preferred_element_type=jnp.float32) * factor
        dq_ref[0, :, cols] = dquery.astype(jnp.bfloat16)
        dkey = (
            lax.dot_general(low, query, (((0,), (0,)), ((), ())), preferred_element_type=jnp.float32)
            * factor
        )
        dvalue = lax.dot_general(
            probs.astype(jnp.bfloat16),
            dcontext,
            (((0,), (0,)), ((), ())),
            preferred_element_type=jnp.float32,
        )
        dkv_ref[:, 0, :, cols] = dkey.astype(jnp.bfloat16).reshape(shards, local, HD)
        dkv_ref[:, 0, :, value_cols] = dvalue.astype(jnp.bfloat16).reshape(shards, local, HD)


def attend(start, lengths, terms, queries, keyvals):
    batch, rows, width = queries.shape
    shards, _, local, double = keyvals.shape
    block = pl.BlockSpec((1, rows, width), lambda b: (b, 0, 0))
    wide = pl.BlockSpec((shards, 1, local, double), lambda b: (0, b, 0, 0))
    return pl.pallas_call(
        attend_kernel,
        grid=(batch,),
        out_shape=jax.ShapeDtypeStruct(queries.shape, jnp.bfloat16),
        in_specs=[SMEM, SMEM, SMEM, block, wide],
        out_specs=block,
        compiler_params=pltpu.CompilerParams(vmem_limit_bytes=VMEM_LIMIT),
        name="attend",
    )(start, lengths, terms, queries, keyvals)


def attend_back(start, lengths, terms, queries, keyvals, dcontext):
    batch, rows, width = queries.shape
    shards, _, local, double = keyvals.shape
    keys = shards * local
    block = pl.BlockSpec((1, rows, width), lambda b: (b, 0, 0))
    wide = pl.BlockSpec((shards, 1, local, double), lambda b: (0, b, 0, 0))
    heads = pl.BlockSpec((1, 2 * H, keys), lambda b: (b, 0, 0))
    return pl.pallas_call(
        attend_back_kernel,
        grid=(batch,),
        out_shape=[
            jax.ShapeDtypeStruct(queries.shape, jnp.bfloat16),
            jax.ShapeDtypeStruct(keyvals.shape, jnp.bfloat16),
            jax.ShapeDtypeStruct((batch, 2 * H, keys), jnp.float32),
        ],
        in_specs=[SMEM, SMEM, SMEM, block, wide, block],
        out_specs=[block, wide, heads],
        compiler_params=pltpu.CompilerParams(vmem_limit_bytes=VMEM_LIMIT),
        name="attend_back",
    )(start, lengths, terms, queries, keyvals, dcontext)


def depth_kernel(taps, padded_ref, weight_ref, out_ref, wide):
    rows = out_ref.shape[1]
    wide[...] = padded_ref[0].astype(jnp.float32)
    shift = HALO - taps // 2
    total = wide[shift : shift + rows, :] * weight_ref[0:1, :]
    for tap in range(1, taps):
        total = total + wide[shift + tap : shift + tap + rows, :] * weight_ref[tap : tap + 1, :]
    out_ref[0] = total


def depth_back_kernel(
    taps, padded_ref, dlow_ref, dhigh_ref, ddepth_ref, weight_ref, dgated_ref, grad_ref, wide, dwide
):
    rows = ddepth_ref.shape[1]
    wide[...] = padded_ref[0].astype(jnp.float32)
    ddepth = ddepth_ref[0]
    dwide[0:HALO, :] = dlow_ref[0].astype(jnp.float32)
    dwide[HALO : HALO + rows, :] = ddepth
    dwide[HALO + rows :, :] = dhigh_ref[0].astype(jnp.float32)
    half = taps // 2
    total = jnp.zeros_like(ddepth)
    for tap in range(taps):
        at = HALO + half - tap
        total = total + dwide[at : at + rows, :] * weight_ref[tap : tap + 1, :]
        at = HALO - half + tap
        grad_ref[0, tap : tap + 1, :] = jnp.sum(
            wide[at : at + rows, :] * ddepth, axis=0, keepdims=True
        )
    grad_ref[0, taps:, :] = jnp.zeros_like(grad_ref[0, taps:, :])
    dgated_ref[0] = total


def lanes(rows, width):
    return pl.BlockSpec((1, rows, 128), lambda b, c: (b, 0, c))


def depth_apply(padded, weights, taps):
    batch, span, width = padded.shape
    rows = span - 2 * HALO
    weight = pl.BlockSpec((weights.shape[0], 128), lambda b, c: (0, c))
    return pl.pallas_call(
        functools.partial(depth_kernel, taps),
        grid=(batch, width // 128),
        out_shape=jax.ShapeDtypeStruct((batch, rows, width), jnp.float32),
        in_specs=[lanes(span, width), weight],
        out_specs=lanes(rows, width),
        scratch_shapes=[pltpu.VMEM((span, 128), jnp.float32)],
        name="depth_apply",
    )(padded, weights)


def depth_back(padded, dlow, dhigh, ddepth, weights, taps):
    batch, span, width = padded.shape
    rows = span - 2 * HALO
    padded_taps = weights.shape[0]
    weight = pl.BlockSpec((padded_taps, 128), lambda b, c: (0, c))
    return pl.pallas_call(
        functools.partial(depth_back_kernel, taps),
        grid=(batch, width // 128),
        out_shape=[
            jax.ShapeDtypeStruct((batch, rows, width), jnp.float32),
            jax.ShapeDtypeStruct((batch, padded_taps, width), jnp.float32),
        ],
        in_specs=[
            lanes(span, width),
            lanes(HALO, width),
            lanes(HALO, width),
            lanes(rows, width),
            weight,
        ],
        out_specs=[lanes(rows, width), lanes(padded_taps, width)],
        scratch_shapes=[
            pltpu.VMEM((span, 128), jnp.float32),
            pltpu.VMEM((span, 128), jnp.float32),
        ],
        name="depth_back",
    )(padded, dlow, dhigh, ddepth, weights)


def edges(block, width):
    count = lax.axis_size("ctx")
    forward = [(i, i + 1) for i in range(count - 1)]
    backward = [(target, source) for source, target in forward]
    low = lax.ppermute(block[:, block.shape[1] - width :], "ctx", forward)
    high = lax.ppermute(block[:, :width], "ctx", backward)
    return low, high


def product(left, right):
    return jnp.dot(left, right, preferred_element_type=jnp.float32)


def product_left(left, right):
    return jnp.dot(left.T, right, preferred_element_type=jnp.float32)


def product_right(left, right):
    return jnp.dot(left, right.T, preferred_element_type=jnp.float32)


def swish(value):
    return value * jax.nn.sigmoid(value)


def swish_slope(value):
    sigma = jax.nn.sigmoid(value)
    return sigma * (1.0 + value * (1.0 - sigma))


def layer_norm(stream, gain):
    centred = stream - jnp.mean(stream, axis=-1, keepdims=True)
    inverse = lax.rsqrt(jnp.mean(centred * centred, axis=-1, keepdims=True) + EPS)
    unit = centred * inverse
    return ((unit * gain).astype(jnp.bfloat16), unit, inverse)


def norm_back(dnormed, unit, inverse, gain):
    scaled = dnormed * gain
    dstream = inverse * (
        scaled
        - jnp.mean(scaled, axis=-1, keepdims=True)
        - unit * jnp.mean(scaled * unit, axis=-1, keepdims=True)
    )
    return (dstream, jnp.sum(dnormed * unit, axis=0))


def per_device(
    tokens,
    lengths,
    cotangent,
    first_up,
    first_down,
    project_in,
    project_out,
    pointwise_in,
    depthwise,
    pointwise_out,
    second_up,
    second_down,
    gains,
    batch_shift,
    head_terms,
):
    micro_count, seqs, local, width = tokens.shape
    batch = micro_count * seqs
    rows = batch * local
    shards = lax.axis_size("fsdp")
    taps = depthwise.shape[1]
    tap_rows = -(-taps // 8) * 8
    gain_count = gains.shape[0]
    bf16 = jnp.bfloat16
    start = (lax.axis_index("ctx") * local).astype(jnp.int32).reshape(1)
    frame_pos = start[0] + lax.iota(jnp.int32, local)
    lengths_flat = lengths.reshape(batch)
    mask = (frame_pos[None, :] < lengths_flat[:, None]).astype(jnp.float32).reshape(rows, 1)
    mask_micro = mask.reshape(micro_count, seqs * local, 1)

    whole_second_up = lax.all_gather(second_up, "fsdp", axis=0, tiled=True)
    whole_second_down = lax.all_gather(second_down, "fsdp", axis=0, tiled=True)
    small = jnp.concatenate([depthwise, gains.T, batch_shift[:, None]], axis=1)
    small_cols = small.shape[1]
    small_width = 256
    small = jnp.pad(small, ((0, 0), (0, small_width - small_cols)))
    gathered = gather(
        [first_up, small, first_down, project_in, project_out, pointwise_in, pointwise_out],
        "fsdp",
        "ctx",
        0,
    )
    gathered = [a.reshape(a.shape[0] * a.shape[1], a.shape[2]) for a in gathered]
    (
        whole_first_up,
        whole_small,
        whole_first_down,
        whole_project_in,
        whole_project_out,
        whole_pointwise_in,
        whole_pointwise_out,
    ) = gathered
    small_rows = whole_small[:, :small_cols].astype(jnp.float32).T
    tap_weights = jnp.pad(small_rows[:taps], ((0, tap_rows - taps), (0, 0)))
    gain_rows = small_rows[taps : taps + gain_count]
    shift_row = small_rows[taps + gain_count]

    stream_in = tokens.reshape(rows, width).astype(jnp.float32)
    normed_first, unit_first, inverse_first = layer_norm(stream_in, gain_rows[0])
    up_first = product(normed_first, whole_first_up)
    act_first = swish(up_first).astype(bf16)
    stream_first = stream_in + 0.5 * product(act_first, whole_first_down)
    normed_attend, unit_attend, inverse_attend = layer_norm(stream_first, gain_rows[1])
    triple = product(normed_attend, whole_project_in).astype(bf16)
    queries = triple[:, :width].reshape(batch, local, width)
    (keyvals,) = gather([triple[:, width:].reshape(batch, local, 2 * width)], "ctx", None, 1)
    context = attend(start, lengths_flat, head_terms, queries, keyvals).reshape(rows, width)
    stream_attend = stream_first + product(context, whole_project_out)
    normed_conv, unit_conv, inverse_conv = layer_norm(stream_attend, gain_rows[2])
    expanded = product(normed_conv, whole_pointwise_in)
    linear = expanded[:, :width]
    gate_sigma = jax.nn.sigmoid(expanded[:, width:])
    gated_low = (linear * gate_sigma * mask).astype(bf16).reshape(batch, local, width)
    low, high = edges(gated_low, HALO)
    padded = jnp.concatenate([low, gated_low, high], axis=1)
    depth = depth_apply(padded, tap_weights, taps).reshape(micro_count, seqs * local, width)

    own_count = jnp.sum(mask_micro, axis=1)
    own_sum = jnp.sum(mask_micro * depth, axis=1)
    own_mean = own_sum / jnp.maximum(own_count, 1.0)
    own_centred = depth - own_mean[:, None, :]
    own_spread = jnp.sum(mask_micro * own_centred * own_centred, axis=1)
    moments = jnp.concatenate(
        [own_sum, own_spread, jnp.broadcast_to(own_count, own_sum.shape)], axis=0
    )
    moment_rows = -(-moments.shape[0] // 8) * 8
    moments = jnp.pad(moments, ((0, moment_rows - moments.shape[0]), (0, 0)))
    moments = channel_merge(moments, functools.partial(merge_moments, micro_count), 2)
    count = moments[2 * micro_count : 3 * micro_count][:, None, :]
    bn_mean = moments[:micro_count][:, None, :] / count
    inverse_bn = lax.rsqrt(moments[micro_count : 2 * micro_count][:, None, :] / count + EPS)
    unit_bn = (depth - bn_mean) * inverse_bn
    shifted = unit_bn * gain_rows[5] + shift_row
    act_conv = swish(shifted).astype(bf16).reshape(rows, width)
    stream_conv = stream_attend + product(act_conv, whole_pointwise_out)
    normed_second, unit_second, inverse_second = layer_norm(stream_conv, gain_rows[3])
    up_second = product(normed_second, whole_second_up)
    act_second = swish(up_second).astype(bf16)
    stream_second = stream_conv + 0.5 * product(act_second, whole_second_down)
    out_low, unit_out, inverse_out = layer_norm(stream_second, gain_rows[4])
    output = out_low.reshape(tokens.shape)

    dout = cotangent.reshape(rows, width).astype(jnp.float32)
    dsecond_stream, gain_out = norm_back(dout, unit_out, inverse_out, gain_rows[4])
    dsecond_low = (0.5 * dsecond_stream).astype(bf16)
    dup_second = (product_right(dsecond_low, whole_second_down) * swish_slope(up_second)).astype(
        bf16
    )
    dtemp, gain_second = norm_back(
        product_right(dup_second, whole_second_up), unit_second, inverse_second, gain_rows[3]
    )
    grad_second_up = product_left(normed_second, dup_second)
    grad_second_down = product_left(act_second, dsecond_low)
    second_pack = jnp.concatenate(
        [
            piece
            for grad in (grad_second_up, grad_second_down)
            for piece in jnp.split(
                grad.astype(bf16).reshape(shards, -1, grad.shape[1]), grad.shape[1] // width, axis=2
            )
        ],
        axis=1,
    )
    second_shard = lax.psum_scatter(second_pack, "fsdp", scatter_dimension=0, tiled=True)
    second_sum = lax.psum(second_shard[0], "ctx")
    up_rows = second_up.shape[0]
    up_blocks = second_up.shape[1] // width
    second_up_sum = jnp.concatenate(
        [second_sum[i * up_rows : (i + 1) * up_rows] for i in range(up_blocks)], axis=1
    ).astype(jnp.float32)
    second_down_sum = second_sum[up_rows * up_blocks :].astype(jnp.float32)

    dconv_stream = dsecond_stream + dtemp
    dconv_low = dconv_stream.astype(bf16)
    dshift = product_right(dconv_low, whole_pointwise_out).reshape(depth.shape) * swish_slope(
        shifted
    )
    own_shift = jnp.sum(dshift, axis=1)
    own_cross = jnp.sum(dshift * unit_bn, axis=1)
    channel = jnp.concatenate([own_shift, own_cross], axis=0)
    channel_rows = -(-channel.shape[0] // 8) * 8
    channel = jnp.pad(channel, ((0, channel_rows - channel.shape[0]), (0, 0)))
    channel = channel_merge(channel, merge_sums, 3)
    sum_shift = channel[:micro_count][:, None, :]
    sum_cross = channel[micro_count : 2 * micro_count][:, None, :]
    ddepth = (
        inverse_bn
        * gain_rows[5]
        * (dshift - mask_micro * sum_shift / count - mask_micro * unit_bn * sum_cross / count)
    ).reshape(batch, local, width)
    dlow, dhigh = edges(ddepth.astype(bf16), HALO)
    dgated, tap_grads = depth_back(padded, dlow, dhigh, ddepth, tap_weights, taps)
    dgated = dgated.reshape(rows, width) * mask
    dexpanded = jnp.concatenate(
        [dgated * gate_sigma, dgated * linear * gate_sigma * (1.0 - gate_sigma)], axis=1
    ).astype(bf16)
    dtemp, gain_conv = norm_back(
        product_right(dexpanded, whole_pointwise_in), unit_conv, inverse_conv, gain_rows[2]
    )
    dattend_stream = dconv_stream + dtemp
    dattend_low = dattend_stream.astype(bf16)
    dcontext = product_right(dattend_low, whole_project_out).astype(bf16)
    dquery, dkeyvals, dheads = attend_back(
        start, lengths_flat, head_terms, queries, keyvals, dcontext.reshape(batch, local, width)
    )
    splits = dkeyvals.shape[0] // 2
    dkeyvals = dkeyvals.reshape(splits, 2, rows, 2 * width)
    (dkeyvals,) = scatter([dkeyvals], "ctx", None, bf16, 4)
    dtriple = jnp.concatenate([dquery.reshape(rows, width), dkeyvals], axis=1)
    dtemp, gain_attend = norm_back(
        product_right(dtriple, whole_project_in), unit_attend, inverse_attend, gain_rows[1]
    )
    dfirst_stream = dattend_stream + dtemp
    dfirst_low = (0.5 * dfirst_stream).astype(bf16)
    dup_first = (product_right(dfirst_low, whole_first_down) * swish_slope(up_first)).astype(bf16)
    dtemp, gain_first = norm_back(
        product_right(dup_first, whole_first_up), unit_first, inverse_first, gain_rows[0]
    )
    grad_tokens = (dfirst_stream + dtemp).astype(bf16).reshape(tokens.shape)

    small_grads = jnp.concatenate(
        [
            jnp.sum(tap_grads, axis=0)[:taps],
            jnp.stack([gain_first, gain_attend, gain_conv, gain_second, gain_out]),
            jnp.sum(own_cross, axis=0, keepdims=True),
            jnp.sum(own_shift, axis=0, keepdims=True),
        ],
        axis=0,
    ).T
    head_row = jnp.sum(dheads, axis=(0, 2)).reshape(1, 1, 2 * H)
    shard_rows = width // shards
    head_block = jnp.pad(
        jnp.broadcast_to(head_row, (shards, 1, 2 * H)),
        ((0, 0), (0, shard_rows - 1), (small_width // 2, small_width // 2 - 2 * H)),
    ).reshape(width, small_width)
    small_block = jnp.pad(small_grads, ((0, 0), (0, small_width - small_cols))) + head_block
    grads = [
        product_left(act_first, dfirst_low),
        product_left(normed_first, dup_first),
        product_left(normed_attend, dtriple),
        product_left(normed_conv, dexpanded),
        product_left(context, dattend_low),
        product_left(act_conv, dconv_low),
        small_block,
    ]
    blocks = [
        g.astype(bf16).reshape(shards // 2, 2, g.shape[0] // shards, g.shape[1]) for g in grads
    ]
    (
        grad_first_down,
        grad_first_up,
        grad_project_in,
        grad_pointwise_in,
        grad_project_out,
        grad_pointwise_out,
        small_sum,
    ) = scatter(blocks, "fsdp", "ctx", jnp.float32, 5)
    heads_at = small_width // 2
    return (
        output,
        grad_tokens,
        grad_first_up,
        grad_first_down,
        grad_project_in,
        grad_project_out,
        grad_pointwise_in,
        small_sum[:, :taps],
        grad_pointwise_out,
        second_up_sum,
        second_down_sum,
        small_sum[:, taps : taps + gain_count].T,
        small_sum[:, taps + gain_count],
        small_sum[0, heads_at : heads_at + 2 * H].reshape(2, H),
    )


def solution(mesh):
    in_specs = (
        P(None, "fsdp", "ctx", None),
        P(None, "fsdp"),
        P(None, "fsdp", "ctx", None),
        P("fsdp", None),
        P("fsdp", None),
        P("fsdp", None),
        P("fsdp", None),
        P("fsdp", None),
        P("fsdp", None),
        P("fsdp", None),
        P("fsdp", None),
        P("fsdp", None),
        P(None, "fsdp"),
        P("fsdp"),
        P(),
    )
    out_specs = (
        P(None, "fsdp", "ctx", None),
        P(None, "fsdp", "ctx", None),
        P("fsdp", None),
        P("fsdp", None),
        P("fsdp", None),
        P("fsdp", None),
        P("fsdp", None),
        P("fsdp", None),
        P("fsdp", None),
        P("fsdp", None),
        P("fsdp", None),
        P(None, "fsdp"),
        P("fsdp"),
        P(),
    )
    return jax.shard_map(
        per_device, mesh=mesh, in_specs=in_specs, out_specs=out_specs, check_vma=False
    )
```

time: 1030 us -> 415 us (0.40); the launches traced: 1010 us -> 413 us
  waiting for transfers between devices: 386 us -> 34.6 us
  Pallas kernels: 0 us -> 262 us
  blocking collectives: 231 us -> 0 us
  local copies, waits for them, and re-layouts: 207 us -> 27.8 us
  matrix products: 91 us -> 42.1 us
  other arithmetic: 61 us -> 23.3 us
  starting transfers between devices: 20 us -> 8.44 us
    pallas_call x0 -> x10, Pallas kernels: none -> 262 us  [the longest x2 102 us: gather(): pl.pallas_call(functools.partial(gather_kernel, count, size, axis, pair),...]
    reduce_scatter x1, waiting for transfers between devices: 221 us -> 0.02 us  [per_device(): lax.psum_scatter(second_pack, 'fsdp', scatter_dimension=0, tiled=True)]
    psum x3 -> x0, blocking collectives: 133 us -> none  [the longest x1 50.5 us: per_device(): sum_shift, sum_cross = lax.psum((grad_shift, grad_gamma), ('fsdp', 'ctx'))]
    all_gather x8 -> x2, waiting for transfers between devices: 107 us -> 0.02 us  [the longest x1 0.02 us: per_device(): whole_second_up = lax.all_gather(second_up, 'fsdp', axis=0, tiled=True)]
    all_gather x3 -> x0, blocking collectives: 98 us -> none  [the longest x1 34.2 us: per_device(): lax.all_gather(pointwise_out, 'fsdp', axis=0, tiled=True)]
    another operation x67 -> x1, local copies, waits for them, and re-layouts: 74.8 us -> 0.64 us  [per_device(): small_sum[0, heads_at:heads_at + 2 * H].reshape(2, H)]
    unnamed x672 -> x161, local copies, waits for them, and re-layouts: 67.3 us -> 15.8 us
    concatenate x3 -> x4, local copies, waits for them, and re-layouts: 25.5 us -> 1.88 us  [the longest x1 1.62 us: per_device(): jnp.concatenate([piece for grad in (grad_second_up, grad_second_down) for...]
  transfers between devices with their start and end apart: 20 -> 8, of which waited for: 7 -> 2; matrix products, arithmetic and copies ran while one was open for 13% -> 16% of each run, Pallas kernels for 0% -> 63%
where the time goes in v1:
time: 415 us; the launch traced here: 413 us
  Pallas kernels  262 us (63%)
  matrix products  42.1 us (10%)
  waiting for transfers between devices  34.6 us (8%)
  local copies, waits for them, and re-layouts  27.8 us (7%)
  other arithmetic  23.3 us (6%)
  between operations  14.8 us (4%)
  starting transfers between devices  8.44 us (2%)
    pallas_call x2, Pallas kernels, gather(): pl.pallas_call(functools.partial(gather_kernel, count, size, axis, pair),...  102 us
    pallas_call x2, Pallas kernels, scatter(): pl.pallas_call(functools.partial(scatter_kernel, count, size, axis, pair,...  98 us
    psum x1, waiting for transfers between devices, per_device(): second_sum = lax.psum(second_shard[0], 'ctx')  32 us
    pallas_call x2, Pallas kernels, channel_merge(): pl.pallas_call(functools.partial(channel_kernel, merge, sizes, axes), out...  28.7 us
    unnamed x161, local copies, waits for them, and re-layouts  15.8 us
    dot_general x8, matrix products, product_right(): return jnp.dot(left, right.T, preferred_element_type=jnp.float32)  15.3 us
    dot_general x8, matrix products, product(): return jnp.dot(left, right, preferred_element_type=jnp.float32)  14 us
    pallas_call x1, Pallas kernels, attend_back(): pl.pallas_call(attend_back_kernel, grid=(batch,), out_shape=[jax.ShapeDty...  13.2 us
  transfers between devices with their start and end apart: 8, of which 2 were waited for; matrix products, arithmetic and copies ran while one was open for 16% of the time, Pallas kernels for 63%

profile of v1, /device:TPU:0, one launch (start us, length us, event | category | flops | bytes accessed | tf_op | source)
XLA Modules:
  0.0 412.9 jit_solution(1542335491525336843)
XLA Ops:
  15.1 85.1 %gather_fsdp.1 = (bf16[8,64,2048]{2,1,0:T(8,128)(2,1)}, bf16[8,64,256]{2,1,0:T(8,128)(2,1)}, bf16[8,256,512]{2,1,0:T(8,128)(2,1)}, bf16[8,64,1536]{2,1,0:T(8,128...) custom-call(bf16[64,2048]{1,0:T(8,128)(2,1)} %refs_0_.1, ...), custom_call_target="tpu_custom_call" | custom-call | tf_op jit(solution)/shard_map/gather_fsdp/pallas_call | solution.py:164
  101.5 2.5 fusion.54
  108.4 17.3 %gather_ctx.1.kv_ref = bf16[4,2,128,1024]{3,2,1,0:T(8,128)(2,1)} custom-call(bf16[2,128,1024]{2,1,0:T(8,128)(2,1)} %bitcast.153), custom_call_target="tpu_custom_call" | custom-call | tf_op jit(solution)/shard_map/gather_ctx/pallas_call | solution.py:164
  125.8 8.6 %attend.1 = bf16[2,128,512]{2,1,0:T(8,128)(2,1)} custom-call(s32[1]{0:T(128)} %bitcast.9.start_ref, s32[2]{0:T(128)} %bitcast.203, f32[2,8]{1,0:T(2,128)} %terms_ref.3, bf16[2,128,512]{2,1,0:T(8,128)(2,1)} %bitcast.144, bf16[4,2,128,1024]{3,2,1,0:T(8,128)(2,1)} %gather_ctx.1.kv_ref), custom_call_target="tpu_custom_call" | custom-call | tf_op jit(solution)/shard_map/attend/pallas_call | solution.py:513
  136.8 2.3 collective-permute-start
  143.5 5.0 %depth_apply.1 = f32[2,128,512]{2,1,0:T(8,128)} custom-call(bf16[2,160,512]{2,1,0:T(8,128)(2,1)} %pad_maximum_fusion.6.padded_ref, f32[32,512]{1,0:T(8,128)} %slice_select_fusion.weight_ref), custom_call_target="tpu_custom_call" | custom-call | tf_op jit(solution)/shard_map/depth_apply/pallas_call | solution.py:586
  151.6 15.4 %channel_merge_2.1 = f32[8,512]{1,0:T(8,128)} custom-call(f32[8,512]{1,0:T(8,128)} %pad.28.in_ref), custom_call_target="tpu_custom_call" | custom-call | tf_op jit(solution)/shard_map/channel_merge_2/pallas_call | solution.py:421
  171.0 3.7 fusion.42
  174.6 3.1 fusion.53
  188.5 3.5 multiply_reduce_fusion
  195.8 13.2 %channel_merge_3.1 = f32[8,512]{1,0:T(8,128)} custom-call(f32[8,512]{1,0:T(8,128)} %select_maximum_fusion.in_ref), custom_call_target="tpu_custom_call" | custom-call | tf_op jit(solution)/shard_map/channel_merge_3/pallas_call | solution.py:421
  209.8 2.1 fusion.43
  213.2 3.3 collective-permute-start.2
  218.2 6.0 %depth_back.1 = (f32[2,128,512]{2,1,0:T(8,128)}, f32[2,32,512]{2,1,0:T(8,128)}) custom-call(bf16[2,160,512]{2,1,0:T(8,128)(2,1)} %pad_maximum_fusion.6.padded_ref, bf16[2,16,512]{2,1,0:T(8,128)(2,1)} %copy-done.41, bf16[2,16,512]{2,1,0:T(8,128)(2,1)} %copy-done.40, f32[2,128,512]{2,1,0:T(8,128)} %get-tuple-element.141.ddepth_ref, ...), custom_call_target="tpu_custom_call" | custom-call | tf_op jit(solution)/shard_map/depth_back/pallas_call | solution.py:602
  225.5 2.1 multiply_reduce_fusion.1
  228.9 13.2 %attend_back.1 = (bf16[2,128,512]{2,1,0:T(8,128)(2,1)}, bf16[4,2,128,1024]{3,2,1,0:T(8,128)(2,1)}, f32[2,16,512]{2,1,0:T(8,128)}) custom-call(s32[1]{0:T(128)} %bitcast.9.start_ref, s32[2]{0:T(128)} %bitcast.204, f32[2,8]{1,0:T(2,128)} %terms_ref.3, bf16[2,128,512]{2,1,0:T(8,128)(2,1)} %bitcast.145, bf16[4,2,128,1024]{3,2,1,0:T(8,128)(2,1)} %gather_ctx.1.kv_ref, ...), custom_call_target="tpu_custom_call" | custom-call | tf_op jit(solution)/shard_map/attend_back/pallas_call | solution.py:531
  242.2 21.1 %scatter_ctx.1 = bf16[256,1024]{1,0:T(8,128)(2,1)} custom-call(bf16[2,2,256,1024]{3,2,1,0:T(8,128)(2,1)} %bitcast.148), custom_call_target="tpu_custom_call" | custom-call | tf_op jit(solution)/shard_map/scatter_ctx/pallas_call | solution.py:350
  263.5 2.5 multiply_reduce_fusion.2
  269.2 2.2 multiply_reduce_fusion.3
  273.6 2.7 convolution_convert_fusion.6
  278.3 2.1 convolution_convert_fusion.2
  280.4 2.1 convolution_convert_fusion.3
  282.6 76.9 %scatter_fsdp.1 = (f32[256,512]{1,0:T(8,128)}, f32[64,2048]{1,0:T(8,128)}, f32[64,1536]{1,0:T(8,128)}, f32[64,1024]{1,0:T(8,128)}, f32[64,512]{1,0:T(8,128)}, /*index=5*/f32[64,512]{1,0:T(8,128)}, f32[64,256]{1,0:T(8,128)}) custom-call(bf16[4,2,256,512]{3,2,1,0:T(8,128)(2,1)} %bitcast.157, bf16[4,2,64,2048]{3,2,1,0:T(8,128)(2,1)} %bitcast.134, ...), custom_call_target="tpu_custom_call" | custom-call | tf_op jit(solution)/shard_map/scatter_fsdp/pallas_call | solution.py:350
  366.3 32.0 %all-reduce.7.cloned.1.call-done = bf16[512,512]{1,0:T(8,128)(2,1)} async-done(((bf16[512,512]{1,0:T(8,128)(2,1)}), bf16[512,512]{1,0:T(8,128)(2,1)}) %all-reduce.7.cloned.1.call-update) | async-done | bytes 524304 | tf_op jit(solution)/shard_map/psum | solution.py:797
  (267 shorter events, 70.1 us)
Async XLA Ops:
  7.2 94.2 %copy-start.1 = (bf16[2,1,128,512]{3,2,1,0:T(8,128)(2,1)S(1)}, bf16[2,1,128,512]{3,2,1,0:T(8,128)(2,1)}, u32[]{:S(2)}) copy-start(bf16[2,1,128,512]{3,2,1,0:T(8,128)(2,1)} %param.15) | copy-start | bytes 786436
  7.2 163.8 %all-gather.3.cloned.1.call-start = ((), (), s32[]{:S(2)}) async-start(), calls=%async_computation.1 | async-start | bytes 2359296 | tf_op jit(solution)/shard_map/all_gather | solution.py:703
  7.9 166.7 %all-gather.5.cloned.1.call-start = ((), (), s32[]{:S(2)}) async-start(), calls=%async_computation.2 | async-start | bytes 2359296 | tf_op jit(solution)/shard_map/all_gather | solution.py:704
  8.7 356.6 %reduce-scatter.2.cloned.1.call-start = ((), (), s32[]{:S(2)}) async-start(), calls=%async_computation.3 | async-start | bytes 4718592 | tf_op jit(solution)/shard_map/reduce_scatter | solution.py:796
  101.3 126.3 %copy-start.42 = (f32[1,512]{1,0:T(1,128)}, f32[1,512]{1,0:T(1,128)S(1)}, u32[]{:S(2)}) copy-start(f32[1,512]{1,0:T(1,128)S(1)} %get-tuple-element.163) | copy-start | bytes 6148
  108.4 26.0 %copy-start.7 = (bf16[8,64,512]{2,1,0:T(8,128)(2,1)S(1)}, bf16[8,64,512]{2,1,0:T(8,128)(2,1)}, u32[]{:S(2)}) copy-start(bf16[8,64,512]{2,1,0:T(8,128)(2,1)} %get-tuple-element.37) | copy-start | bytes 1572868
  135.8 91.8 %copy-start.46 = (f32[256]{0:T(256)}, f32[256]{0:T(256)S(1)}, u32[]{:S(2)}) copy-start(f32[256]{0:T(256)S(1)} %broadcast_multiply_fusion.12) | copy-start | bytes 3076
  136.0 91.6 %copy-start.53 = (f32[256]{0:T(256)}, f32[256]{0:T(256)S(1)}, u32[]{:S(2)}) copy-start(f32[256]{0:T(256)S(1)} %add_rsqrt_fusion.3) | copy-start | bytes 3076
  136.8 4.9 %collective-permute-start = (bf16[2,16,512]{2,1,0:T(8,128)(2,1)S(1)}, bf16[2,16,512]{2,1,0:T(8,128)(2,1)S(1)}, u32[]{:S(2)}, u32[]{:S(2)}) collective-permute-start(bf16[2,16,512]{2,1,0:T(8,128)(2,1)S(1)} %get-tuple-element.157), channel_id=1, source_target_pairs={{0,1},{1,2},{2,3},{4,5},{5,6},{6,7},{8,9},{9,10},{10,11},{12,13},{... | collective-permute-start | bytes 98312 | tf_op jit(solution)/shard_map/ppermute | solution.py:629
  139.0 3.7 collective-permute-start.1
  188.4 210.0 %all-reduce.7.cloned.1.call-start = ((), (), s32[]{:S(2)}) async-start(), calls=%async_computation.4 | async-start | bytes 1048576 | tf_op jit(solution)/shard_map/psum | solution.py:797
  211.9 5.7 %collective-permute-start.3 = (bf16[2,16,512]{2,1,0:T(8,128)(2,1)S(1)}, bf16[2,16,512]{2,1,0:T(8,128)(2,1)S(1)}, u32[]{:S(2)}, u32[]{:S(2)}) collective-permute-start(bf16[2,16,512]{2,1,0:T(8,128)(2,1)S(1)} %get-tuple-element.155), channel_id=1, source_target_pairs={{1,0},{2,1},{3,2},{5,4},{6,5},{7,6},{9,8},{10,9},{11,10},{13,12},{... | collective-permute-start | bytes 98312 | tf_op jit(solution)/shard_map/ppermute | solution.py:630
  213.2 4.4 %collective-permute-start.2 = (bf16[2,16,512]{2,1,0:T(8,128)(2,1)S(1)}, bf16[2,16,512]{2,1,0:T(8,128)(2,1)S(1)}, u32[]{:S(2)}, u32[]{:S(2)}) collective-permute-start(bf16[2,16,512]{2,1,0:T(8,128)(2,1)S(1)} %get-tuple-element.156), channel_id=1, source_target_pairs={{0,1},{1,2},{2,3},{4,5},{5,6},{6,7},{8,9},{9,10},{10,11},{12,13},{... | collective-permute-start | bytes 98312 | tf_op jit(solution)/shard_map/ppermute | solution.py:629
  228.9 34.5 %copy-start.36 = (f32[2,32,512]{2,1,0:T(8,128)S(1)}, f32[2,32,512]{2,1,0:T(8,128)}, u32[]{:S(2)}) copy-start(f32[2,32,512]{2,1,0:T(8,128)} %get-tuple-element.43) | copy-start | bytes 393220
  242.1 21.3 %copy-start.44 = (f32[1,512]{1,0:T(1,128)S(1)}, f32[1,512]{1,0:T(1,128)}, u32[]{:S(2)}) copy-start(f32[1,512]{1,0:T(1,128)} %copy-done.43) | copy-start | bytes 6148
  282.6 82.7 %copy-start.68 = (f32[256]{0:T(256)S(1)}, f32[256]{0:T(256)}, u32[]{:S(2)}) copy-start(f32[256]{0:T(256)} %get-tuple-element.133) | copy-start | bytes 3076
  282.6 82.7 %copy-start.67 = (f32[256]{0:T(256)S(1)}, f32[256]{0:T(256)}, u32[]{:S(2)}) copy-start(f32[256]{0:T(256)} %get-tuple-element.134) | copy-start | bytes 3076
  282.6 82.8 %copy-start.29 = (f32[256,512]{1,0:T(8,128)S(1)}, f32[256,512]{1,0:T(8,128)}, u32[]{:S(2)}) copy-start(f32[256,512]{1,0:T(8,128)} %get-tuple-element.188) | copy-start | bytes 1572868
  282.6 82.8 %copy-start.52 = (f32[1,512]{1,0:T(1,128)S(1)}, f32[1,512]{1,0:T(1,128)}, u32[]{:S(2)}) copy-start(f32[1,512]{1,0:T(1,128)} %copy-done.50) | copy-start | bytes 6148
  282.6 82.8 %copy-start.61 = (f32[256]{0:T(256)S(1)}, f32[256]{0:T(256)}, u32[]{:S(2)}) copy-start(f32[256]{0:T(256)} %get-tuple-element.172) | copy-start | bytes 3076
  282.6 82.8 %copy-start.63 = (f32[256]{0:T(256)S(1)}, f32[256]{0:T(256)}, u32[]{:S(2)}) copy-start(f32[256]{0:T(256)} %get-tuple-element.170) | copy-start | bytes 3076
  365.3 36.7 %copy-start.31 = (f32[64,2048]{1,0:T(8,128)S(1)}, f32[64,2048]{1,0:T(8,128)}, u32[]{:S(2)}) copy-start(f32[64,2048]{1,0:T(8,128)} %get-tuple-element.207) | copy-start | bytes 1572868
  365.4 37.4 %copy-start.30 = (f32[256,512]{1,0:T(8,128)S(1)}, f32[256,512]{1,0:T(8,128)}, u32[]{:S(2)}) copy-start(f32[256,512]{1,0:T(8,128)} %get-tuple-element.208) | copy-start | bytes 1572868
  366.3 37.3 %copy-start.32 = (f32[64,1536]{1,0:T(8,128)S(1)}, f32[64,1536]{1,0:T(8,128)}, u32[]{:S(2)}) copy-start(f32[64,1536]{1,0:T(8,128)} %get-tuple-element.209) | copy-start | bytes 1179652
  (57 other events, 299.7 us)
Sparse Core Ops, SparseCore 0:
  10.1 75.9 all-gather.2
  88.2 50.4 all-gather.4
  188.5 90.6 reduce-scatter.1
  365.5 32.8 all-reduce.6

commit v2 on v1

--- a/solution.py
+++ b/solution.py
@@ -48,316 +48,349 @@
     )
 
 
-def gather_kernel(count, size, axis, pair, *refs):
-    ins, outs = refs[:count], refs[count : 2 * count]
-    keep, zs, zr, ys, yr, cs, cr = refs[2 * count :]
-    me = lax.axis_index(axis)
-    highs = size // 2
-    low, high = lax.rem(me, 2), lax.div(me, 2)
-    partner = other_of(me)
-
-    def part(ref, mine=True):
-        if pair is None:
-            return ref
-        width = ref.shape[-1] // 2
-        side = lax.rem(lax.axis_index(pair), 2)
-        start = pl.multiple_of((side if mine else 1 - side) * width, width)
-        return ref.at[:, pl.ds(start, width)]
-
-    peers = [{axis: 2 * rotated(high, d, highs) + low} for d in range(1, highs)]
-    peers.append({axis: partner})
-    if pair is not None:
-        pair_to = {pair: other_of(lax.axis_index(pair))}
-        peers.append(pair_to)
-    greet(peers)
-
-    def origin(d):
-        return 2 * rotated(high, -d, highs)
-
-    def along(a, d, landed=False):
-        place = origin(d) + low if landed else me
-        return send(
-            part(ins[a]),
-            part(outs[a].at[place]),
-            zs.at[a, d],
-            zr.at[a, d],
-            {axis: 2 * rotated(high, d, highs) + low},
-        )
-
-    def across_first(a, landed=False):
-        place = partner if landed else me
-        return send(part(ins[a]), part(outs[a].at[place]), ys.at[a, 0], yr.at[a, 0], {axis: partner})
-
-    def across(a, d, landed=False):
-        place = origin(d) + (1 - low if landed else low)
-        return send(
-            part(outs[a].at[origin(d) + low]),
-            part(outs[a].at[place]),
-            ys.at[a, d],
-            yr.at[a, d],
-            {axis: partner},
-        )
-
-    def hand(a, place, landed=False):
-        return send(
-            part(outs[a].at[place]),
-            part(outs[a].at[place], not landed),
-            cs.at[a, place],
-            cr.at[a, place],
-            pair_to,
-        )
-
-    def steps(first, last, body):
-        def step(i, carry):
-            body(i)
-            return carry
-
-        lax.fori_loop(first, last, step, 0)
-
-    def local(a):
-        return pltpu.make_async_copy(ins[a], outs[a].at[me], keep.at[a])
-
-    for a in range(count):
-        steps(1, highs, lambda d: along(a, d).start())
-        across_first(a).start()
-    for a in range(count):
-        local(a).start()
-
-    def second(a):
-        across_first(a, True).wait_recv()
+def steps(first, last, body):
+    def step(i, carry):
+        body(i)
+        return carry
+
+    lax.fori_loop(first, last, step, 0)
+
+
+def dma(*shape):
+    return pltpu.SemaphoreType.DMA(shape)
+
+
+def staged(count, stages):
+    return [
+        functools.partial(stage, step - index)
+        for step in range(count + len(stages) - 1)
+        for index, stage in enumerate(stages)
+        if 0 <= step - index < count
+    ]
+
+
+class Gather:
+    def __init__(self, arrays, axis, pair=None, shares=None):
+        self.inputs, self.axis, self.pair = arrays, axis, pair
+        count, size = len(arrays), lax.axis_size(axis)
+        places = 1 if pair is None else lax.axis_size(pair) // 2
+        self.size, self.places = size, places
+        self.used = [places if shares and shares[a] else 1 for a in range(count)]
+        highs, most = size // 2, max(self.used)
+        self.in_specs = [VMEM] * count
+        self.out_specs = [ANY] * count
+        self.outputs = [jax.ShapeDtypeStruct((size,) + a.shape, a.dtype) for a in arrays]
+        self.scratch = [dma(count)] + [dma(count, highs)] * 4
         if pair is not None:
-            hand(a, partner).start()
-
-        def one(d):
-            across(a, d, True).wait_recv()
+            self.scratch += [dma(count, size, most)] * 2
+            self.scratch += [dma(count, size, most)] * 2
+
+    def bind(self, ins, outs, scratch):
+        axis, pair, size, places, used = self.axis, self.pair, self.size, self.places, self.used
+        count = len(ins)
+        keep, zs, zr, ys, yr = scratch[:5]
+        me = lax.axis_index(axis)
+        highs = size // 2
+        low, high = lax.rem(me, 2), lax.div(me, 2)
+        partner = other_of(me)
+        self.peers = {(axis, d): {axis: 2 * rotated(high, d, highs) + low} for d in range(1, highs)}
+        self.peers[axis, 0] = {axis: partner}
+        if pair is not None:
+            cs, cr, xs, xr = scratch[5:]
+            spot = lax.axis_index(pair)
+            side, place = lax.rem(spot, 2), lax.div(spot, 2)
+            pair_to = {pair: other_of(spot)}
+            self.peers[pair, 0] = pair_to
+            if max(used) > 1:
+                for e in range(1, places):
+                    self.peers[pair, e] = {pair: 2 * rotated(place, e, places) + side}
+
+        def part(a, ref, at=None, mine=True):
+            if pair is None:
+                return ref
+            width = ref.shape[-1] // (2 * used[a])
+            if at is None:
+                at = place if used[a] > 1 else 0
+            index = 2 * at + (side if mine else 1 - side)
+            return ref.at[:, pl.ds(pl.multiple_of(index * width, width), width)]
+
+        def origin(d):
+            return 2 * rotated(high, -d, highs)
+
+        def along(a, d, landed=False):
+            spot_to = origin(d) + low if landed else me
+            return send(
+                part(a, ins[a]),
+                part(a, outs[a].at[spot_to]),
+                zs.at[a, d],
+                zr.at[a, d],
+                {axis: 2 * rotated(high, d, highs) + low},
+            )
+
+        def across_first(a, landed=False):
+            return send(
+                part(a, ins[a]),
+                part(a, outs[a].at[partner if landed else me]),
+                ys.at[a, 0],
+                yr.at[a, 0],
+                {axis: partner},
+            )
+
+        def across(a, d, landed=False):
+            return send(
+                part(a, outs[a].at[origin(d) + low]),
+                part(a, outs[a].at[origin(d) + (1 - low if landed else low)]),
+                ys.at[a, d],
+                yr.at[a, d],
+                {axis: partner},
+            )
+
+        def slot(a):
+            return place if used[a] > 1 else 0
+
+        def over(a, block, e, landed=False):
+            at = rotated(place, -e, places) if landed else place
+            return send(
+                part(a, outs[a].at[block]),
+                part(a, outs[a].at[block], at),
+                xs.at[a, block, e],
+                xr.at[a, block, e],
+                {pair: 2 * rotated(place, e, places) + side},
+            )
+
+        def hand(a, block, at, landed=False):
+            return send(
+                part(a, outs[a].at[block], at),
+                part(a, outs[a].at[block], at, not landed),
+                cs.at[a, block, at],
+                cr.at[a, block, at],
+                pair_to,
+            )
+
+        def local(a):
+            return pltpu.make_async_copy(ins[a], outs[a].at[me], keep.at[a])
+
+        def spread(a, block):
             if pair is not None:
-                hand(a, origin(d) + 1 - low).start()
-
-        steps(1, highs, one)
-
-    for a in range(count):
-
-        def one(d):
-            along(a, d, True).wait_recv()
-            across(a, d).start()
-            if pair is not None:
-                hand(a, origin(d) + low).start()
-
-        steps(1, highs, one)
-        if a > 0:
-            second(a - 1)
-    second(count - 1)
-    for a in range(count):
+                for e in range(1, used[a]):
+                    over(a, block, e).start()
+                hand(a, block, slot(a)).start()
+
+        def start():
+            for a in range(count):
+                steps(1, highs, lambda d: along(a, d).start())
+                across_first(a).start()
+            for a in range(count):
+                local(a).start()
+
+        def first(a):
+            def one(d):
+                along(a, d, True).wait_recv()
+                across(a, d).start()
+                spread(a, origin(d) + low)
+
+            steps(1, highs, one)
+
+        def second(a):
+            across_first(a, True).wait_recv()
+            spread(a, partner)
+
+            def one(d):
+                across(a, d, True).wait_recv()
+                spread(a, origin(d) + 1 - low)
+
+            steps(1, highs, one)
+
+        def third(a):
+            for e in range(1, used[a]):
+
+                def one(i):
+                    block = rotated(me, i, size)
+                    over(a, block, e, True).wait_recv()
+                    hand(a, block, rotated(place, -e, places)).start()
+
+                steps(1, size, one)
+
+        def finish():
+            for a in range(count):
+                if pair is not None:
+                    for e in range(used[a]):
+                        at = rotated(place, -e, places) if used[a] > 1 else 0
+                        steps(1, size, lambda i: hand(a, rotated(me, i, size), at, True).wait_recv())
+                        steps(1, size, lambda i: hand(a, rotated(me, i, size), at).wait_send())
+                        if e > 0:
+                            steps(1, size, lambda i: over(a, rotated(me, i, size), e).wait_send())
+                steps(1, highs, lambda d: along(a, d).wait_send())
+                across_first(a).wait_send()
+                steps(1, highs, lambda d: across(a, d).wait_send())
+                local(a).wait()
+
+        self.start, self.finish = start, finish
+        self.steps = staged(count, [first, second, third] if max(used) > 1 else [first, second])
+
+
+class Scatter:
+    def __init__(self, arrays, axis, pair, dtype):
+        self.inputs, self.axis, self.pair = arrays, axis, pair
+        count = len(arrays)
+        self.size = 1 if axis is None else lax.axis_size(axis)
+        self.pair_size = 1 if pair is None else lax.axis_size(pair)
+        highs, places = self.size // 2, self.pair_size // 2
+        split = 1 if pair is None else 2
+        low_type = jnp.bfloat16
+        tail = [(a.shape[-2], a.shape[-1] // split) for a in arrays]
+        self.in_specs = [VMEM] * count
+        self.out_specs = [VMEM] * count
+        self.outputs = [jax.ShapeDtypeStruct(a.shape[-2:], dtype) for a in arrays]
+        self.scratch = []
         if pair is not None:
-            steps(1, size, lambda i: hand(a, rotated(me, i, size), True).wait_recv())
-            steps(1, size, lambda i: hand(a, rotated(me, i, size)).wait_send())
-        steps(1, highs, lambda d: along(a, d).wait_send())
-        across_first(a).wait_send()
-        steps(1, highs, lambda d: across(a, d).wait_send())
-        local(a).wait()
-
-
-def gather(arrays, axis, pair, ident):
-    count, size = len(arrays), lax.axis_size(axis)
-    highs = size // 2
-    dma = pltpu.SemaphoreType.DMA
-    return pl.pallas_call(
-        functools.partial(gather_kernel, count, size, axis, pair),
-        out_shape=[jax.ShapeDtypeStruct((size,) + a.shape, a.dtype) for a in arrays],
-        in_specs=[VMEM] * count,
-        out_specs=[ANY] * count,
-        scratch_shapes=[
-            dma((count,)),
-            dma((count, highs)),
-            dma((count, highs)),
-            dma((count, highs)),
-            dma((count, highs)),
-            dma((count, size)),
-            dma((count, size)),
-        ],
-        compiler_params=pltpu.CompilerParams(
-            collective_id=ident, has_side_effects=True, vmem_limit_bytes=VMEM_LIMIT
-        ),
-        name="gather_" + axis,
-    )(*arrays)
-
-
-def scatter_kernel(count, size, axis, pair, pair_size, *refs):
-    ins, outs = refs[:count], refs[count : 2 * count]
-    scratch = refs[2 * count :]
-    if pair is None:
+            leads = () if axis is None else (highs, 2)
+            self.scratch += [pltpu.VMEM(leads + t, low_type) for t in tail]
+            self.scratch += [pltpu.VMEM((places,) + t, low_type) for t in tail]
+            self.scratch += [dma(count)] * 2 + [dma(count, places)] * 2 + [dma(count)] * 2
+        if axis is not None:
+            self.scratch += [pltpu.VMEM((highs,) + t, low_type) for t in tail]
+            self.scratch += [pltpu.VMEM((highs - 1,) + t, low_type) for t in tail]
+            self.scratch += [dma(count)] * 2 + [dma(count, highs)] * 2
+
+    def bind(self, ins, outs, scratch):
+        axis, pair, size, places = self.axis, self.pair, self.size, self.pair_size // 2
+        count = len(ins)
+        self.peers = {}
         halves = ins
-        rest = scratch
-    else:
-        halves = scratch[:count]
-        rest = scratch[count:]
-    lows, highs_in = rest[:count], rest[count : 2 * count]
-    rest = rest[2 * count :]
-    if pair is not None:
-        cross = rest[:count]
-        rest = rest[count:]
-        cs, cr, xs, xr, fs, fr = rest[:6]
-        rest = rest[6:]
-    ys, yr, zs, zr = rest
-    me = lax.axis_index(axis)
-    highs = size // 2
-    low, high = lax.rem(me, 2), lax.div(me, 2)
-    partner = {axis: other_of(me)}
-    peers = [{axis: 2 * rotated(high, d, highs) + low} for d in range(1, highs)]
-    peers.append(partner)
-    if pair is not None:
-        spot = lax.axis_index(pair)
-        side, place = lax.rem(spot, 2), lax.div(spot, 2)
-        places = pair_size // 2
-        pair_to = {pair: other_of(spot)}
-        peers.append(pair_to)
-        for e in range(1, places):
-            peers.append({pair: 2 * rotated(place, e, places) + side})
-    greet(peers)
-
-    def columns(a, mine):
-        width = halves[a].shape[-1]
-        return pl.ds(pl.multiple_of((side if mine else 1 - side) * width, width), width)
-
-    def first(a):
-        return send(ins[a].at[:, :, :, columns(a, False)], halves[a], cs.at[a], cr.at[a], pair_to)
-
-    def across(a):
-        return send(halves[a].at[:, 1 - low], lows[a], ys.at[a], yr.at[a], partner)
-
-    def along(a, d):
-        to = rotated(high, d, highs)
-        return send(
-            lows[a].at[to],
-            highs_in[a].at[d - 1],
-            zs.at[a, d - 1],
-            zr.at[a, d - 1],
-            {axis: 2 * to + low},
-        )
-
-    def over(a, e, landed=False):
-        slot = rotated(place, -e, places) if landed else place
-        return send(
-            cross[a].at[place],
-            cross[a].at[slot],
-            xs.at[a, e - 1],
-            xr.at[a, e - 1],
-            {pair: 2 * rotated(place, e, places) + side},
-        )
-
-    def final(a, landed=False):
-        return send(
-            outs[a].at[:, columns(a, True)],
-            outs[a].at[:, columns(a, not landed)],
-            fs.at[a],
-            fr.at[a],
-            pair_to,
-        )
-
-    def steps(first_step, last, body):
-        def step(i, carry):
-            body(i)
-            return carry
-
-        lax.fori_loop(first_step, last, step, 0)
-
-    def stage_first(a):
-        first(a).wait_recv()
-
-        def one(i):
-            for j in range(2):
-                own = ins[a][i, j, :, columns(a, True)].astype(jnp.float32)
-                halves[a][i, j] = (own + halves[a][i, j].astype(jnp.float32)).astype(jnp.bfloat16)
-
-        steps(0, highs, one)
-        across(a).start()
-
-    def stage_across(a):
-        across(a).wait_recv()
-
-        def one(i):
-            own = halves[a][i, low].astype(jnp.float32)
-            lows[a][i] = (own + lows[a][i].astype(jnp.float32)).astype(jnp.bfloat16)
-
-        steps(0, highs, one)
-        steps(1, highs, lambda d: along(a, d).start())
-
-    def stage_along(a):
-        steps(1, highs, lambda d: along(a, d).wait_recv())
-
-        def added(d, total):
-            return total + highs_in[a][d - 1].astype(jnp.float32)
-
-        total = lax.fori_loop(1, highs, added, lows[a][high].astype(jnp.float32))
-        if pair is None:
-            outs[a][...] = total.astype(outs[a].dtype)
-            return
-        cross[a][place] = total.astype(jnp.bfloat16)
-        for e in range(1, places):
-            over(a, e).start()
-
-    def stage_over(a):
-        for e in range(1, places):
-            over(a, e, True).wait_recv()
-        total = cross[a][0].astype(jnp.float32)
-        for i in range(1, places):
-            total = total + cross[a][i].astype(jnp.float32)
-        outs[a][:, columns(a, True)] = total
-        final(a).start()
-
-    if pair is None:
-        stages = [stage_across, stage_along]
-        for a in range(count):
+        if pair is not None:
+            halves, cross = scratch[:count], scratch[count : 2 * count]
+            cs, cr, xs, xr, fs, fr = scratch[2 * count : 2 * count + 6]
+            scratch = scratch[2 * count + 6 :]
+            spot = lax.axis_index(pair)
+            side, place = lax.rem(spot, 2), lax.div(spot, 2)
+            pair_to = {pair: other_of(spot)}
+            self.peers[pair, 0] = pair_to
+            for e in range(1, places):
+                self.peers[pair, e] = {pair: 2 * rotated(place, e, places) + side}
+        if axis is not None:
+            lows, highs_in = scratch[:count], scratch[count : 2 * count]
+            ys, yr, zs, zr = scratch[2 * count :]
+            me = lax.axis_index(axis)
+            highs = size // 2
+            low, high = lax.rem(me, 2), lax.div(me, 2)
+            partner = {axis: other_of(me)}
+            for d in range(1, highs):
+                self.peers[axis, d] = {axis: 2 * rotated(high, d, highs) + low}
+            self.peers[axis, 0] = partner
+
+        def columns(a, mine):
+            width = halves[a].shape[-1]
+            return pl.ds(pl.multiple_of((side if mine else 1 - side) * width, width), width)
+
+        def first(a):
+            theirs = columns(a, False)
+            piece = ins[a].at[:, theirs] if axis is None else ins[a].at[:, :, :, theirs]
+            return send(piece, halves[a], cs.at[a], cr.at[a], pair_to)
+
+        def across(a):
+            return send(halves[a].at[:, 1 - low], lows[a], ys.at[a], yr.at[a], partner)
+
+        def along(a, d):
+            to = rotated(high, d, highs)
+            return send(
+                lows[a].at[to],
+                highs_in[a].at[d - 1],
+                zs.at[a, d - 1],
+                zr.at[a, d - 1],
+                {axis: 2 * to + low},
+            )
+
+        def over(a, e, landed=False):
+            slot = rotated(place, -e, places) if landed else place
+            return send(
+                cross[a].at[place],
+                cross[a].at[slot],
+                xs.at[a, e - 1],
+                xr.at[a, e - 1],
+                {pair: 2 * rotated(place, e, places) + side},
+            )
+
+        def final(a, landed=False):
+            return send(
+                outs[a].at[:, columns(a, True)],
+                outs[a].at[:, columns(a, not landed)],
+                fs.at[a],
+                fr.at[a],
+                pair_to,
+            )
+
+        def wide(value):
+            return value.astype(jnp.float32)
+
+        def stage_first(a):
+            first(a).wait_recv()
+            if axis is None:
+                total = wide(ins[a][:, columns(a, True)]) + wide(halves[a][...])
+                cross[a][place] = total.astype(jnp.bfloat16)
+                for e in range(1, places):
+                    over(a, e).start()
+                return
+
+            def one(i):
+                for j in range(2):
+                    own = wide(ins[a][i, j, :, columns(a, True)])
+                    halves[a][i, j] = (own + wide(halves[a][i, j])).astype(jnp.bfloat16)
+
+            steps(0, highs, one)
             across(a).start()
-    else:
-        stages = [stage_first, stage_across, stage_along, stage_over]
-        for a in range(count):
-            first(a).start()
-    for step in range(count + len(stages) - 1):
-        for index, stage in enumerate(stages):
-            if 0 <= step - index < count:
-                stage(step - index)
-    for a in range(count):
-        across(a).wait_send()
-        steps(1, highs, lambda d: along(a, d).wait_send())
-        if pair is not None:
-            first(a).wait_send()
+
+        def stage_across(a):
+            across(a).wait_recv()
+
+            def one(i):
+                lows[a][i] = (wide(halves[a][i, low]) + wide(lows[a][i])).astype(jnp.bfloat16)
+
+            steps(0, highs, one)
+            steps(1, highs, lambda d: along(a, d).start())
+
+        def stage_along(a):
+            steps(1, highs, lambda d: along(a, d).wait_recv())
+
+            def added(d, total):
+                return total + wide(highs_in[a][d - 1])
+
+            total = lax.fori_loop(1, highs, added, wide(lows[a][high]))
+            if pair is None:
+                outs[a][...] = total.astype(outs[a].dtype)
+                return
+            cross[a][place] = total.astype(jnp.bfloat16)
             for e in range(1, places):
-                over(a, e).wait_send()
-            final(a, True).wait_recv()
-            final(a).wait_send()
-
-
-def scatter(arrays, axis, pair, dtype, ident):
-    count, size = len(arrays), lax.axis_size(axis)
-    highs = size // 2
-    dma = pltpu.SemaphoreType.DMA
-    low_type = jnp.bfloat16
-    pair_size = 2 if pair is None else lax.axis_size(pair)
-    split = 1 if pair is None else 2
-    tail = [(a.shape[2], a.shape[3] // split) for a in arrays]
-    scratch = []
-    if pair is not None:
-        scratch += [pltpu.VMEM((highs, 2) + t, low_type) for t in tail]
-    scratch += [pltpu.VMEM((highs,) + t, low_type) for t in tail]
-    scratch += [pltpu.VMEM((highs - 1,) + t, low_type) for t in tail]
-    if pair is not None:
-        scratch += [pltpu.VMEM((pair_size // 2,) + t, low_type) for t in tail]
-        others = (count, pair_size // 2)
-        scratch += [dma((count,)), dma((count,)), dma(others), dma(others)]
-        scratch += [dma((count,)), dma((count,))]
-    scratch += [dma((count,)), dma((count,)), dma((count, highs)), dma((count, highs))]
-    return pl.pallas_call(
-        functools.partial(scatter_kernel, count, size, axis, pair, pair_size),
-        out_shape=[jax.ShapeDtypeStruct(a.shape[2:], dtype) for a in arrays],
-        in_specs=[VMEM] * count,
-        out_specs=[VMEM] * count,
-        scratch_shapes=scratch,
-        compiler_params=pltpu.CompilerParams(
-            collective_id=ident, has_side_effects=True, vmem_limit_bytes=VMEM_LIMIT
-        ),
-        name="scatter_" + axis,
-    )(*arrays)
+                over(a, e).start()
+
+        def stage_over(a):
+            for e in range(1, places):
+                over(a, e, True).wait_recv()
+            total = wide(cross[a][0])
+            for i in range(1, places):
+                total = total + wide(cross[a][i])
+            outs[a][:, columns(a, True)] = total
+            final(a).start()
+
+        def start():
+            for a in range(count):
+                (across(a) if pair is None else first(a)).start()
+
+        def finish():
+            for a in range(count):
+                if axis is not None:
+                    across(a).wait_send()
+                    steps(1, highs, lambda d: along(a, d).wait_send())
+                if pair is not None:
+                    first(a).wait_send()
+                    for e in range(1, places):
+                        over(a, e).wait_send()
+                    final(a, True).wait_recv()
+                    final(a).wait_send()
+
+        middle = [] if axis is None else [stage_across, stage_along]
+        stages = middle if pair is None else [stage_first] + middle + [stage_over]
+        self.start, self.finish, self.steps = start, finish, staged(count, stages)
 
 
 def merge_sums(parts):
@@ -378,55 +411,113 @@
     return jnp.concatenate([total[sums], spread, total[counts], total[3 * micro :]], axis=0)
 
 
-def channel_kernel(merge, sizes, axes, in_ref, out_ref, *refs):
-    slots, sums = refs[:2], refs[2]
-    sems = refs[3:]
-    peers = []
-    for axis, size in zip(axes, sizes):
-        for d in range(1, size):
-            peers.append({axis: rotated(lax.axis_index(axis), d, size)})
-    greet(peers)
-    source = in_ref
-    for stage, (axis, size) in enumerate(zip(axes, sizes)):
-        me = lax.axis_index(axis)
-        slot, ss, rs = slots[stage], sems[2 * stage], sems[2 * stage + 1]
-
-        def copy(d, landed=False):
-            place = rotated(me, -d, size) if landed else me
+class Channels:
+    def __init__(self, rows, merge):
+        self.inputs, self.merge = [rows], merge
+        self.axes = ("ctx", "fsdp")
+        self.sizes = tuple(lax.axis_size(axis) for axis in self.axes)
+        self.in_specs, self.out_specs = [VMEM], [VMEM]
+        self.outputs = [jax.ShapeDtypeStruct(rows.shape, rows.dtype)]
+        self.scratch = [pltpu.VMEM((size,) + rows.shape, rows.dtype) for size in self.sizes]
+        self.scratch.append(pltpu.VMEM(rows.shape, rows.dtype))
+        for size in self.sizes:
+            self.scratch += [dma(size), dma(size)]
+
+    def bind(self, ins, outs, scratch):
+        slots, sums, sems = scratch[:2], scratch[2], scratch[3:]
+        self.peers = {}
+        for axis, size in zip(self.axes, self.sizes):
+            me = lax.axis_index(axis)
+            low, high, highs = lax.rem(me, 2), lax.div(me, 2), size // 2
+            for d in range(1, highs):
+                self.peers[axis, d] = {axis: 2 * rotated(high, d, highs) + low}
+            self.peers[axis, 0] = {axis: other_of(me)}
+            for d in range(1, highs):
+                self.peers[axis, -d] = {axis: 2 * rotated(high, d, highs) + 1 - low}
+
+        def source(stage):
+            return ins[0] if stage == 0 else sums
+
+        def copy(stage, d, landed=False):
+            axis, size = self.axes[stage], self.sizes[stage]
+            me = lax.axis_index(axis)
             return send(
-                source, slot.at[place], ss.at[d], rs.at[d], {axis: rotated(me, d, size)}
+                source(stage),
+                slots[stage].at[rotated(me, -d, size) if landed else me],
+                sems[2 * stage].at[d],
+                sems[2 * stage + 1].at[d],
+                {axis: rotated(me, d, size)},
             )
 
-        for d in range(1, size):
-            copy(d).start()
-        slot[me] = source[...]
-        for d in range(1, size):
-            copy(d, True).wait_recv()
-        total = merge([slot[i] for i in range(size)])
-        for d in range(1, size):
-            copy(d).wait_send()
-        target = sums if stage == 0 else out_ref
-        target[...] = total
-        source = sums
-
-
-def channel_merge(rows, merge, ident):
-    axes = ("ctx", "fsdp")
-    sizes = tuple(lax.axis_size(axis) for axis in axes)
-    dma = pltpu.SemaphoreType.DMA
-    scratch = [pltpu.VMEM((size,) + rows.shape, rows.dtype) for size in sizes]
-    scratch.append(pltpu.VMEM(rows.shape, rows.dtype))
-    for size in sizes:
-        scratch += [dma((size,)), dma((size,))]
-    return pl.pallas_call(
-        functools.partial(channel_kernel, merge, sizes, axes),
-        out_shape=jax.ShapeDtypeStruct(rows.shape, rows.dtype),
-        in_specs=[VMEM],
-        out_specs=VMEM,
-        scratch_shapes=scratch,
-        compiler_params=pltpu.CompilerParams(collective_id=ident, has_side_effects=True),
-        name="channel_merge_" + str(ident),
-    )(rows)
+        def begin(stage):
+            for d in range(1, self.sizes[stage]):
+                copy(stage, d).start()
+            slots[stage][lax.axis_index(self.axes[stage])] = source(stage)[...]
+
+        def end(stage):
+            for d in range(1, self.sizes[stage]):
+                copy(stage, d, True).wait_recv()
+            total = self.merge([slots[stage][i] for i in range(self.sizes[stage])])
+            (sums if stage == 0 else outs[0])[...] = total
+
+        def finish():
+            for stage in range(2):
+                for d in range(1, self.sizes[stage]):
+                    copy(stage, d).wait_send()
+
+        def middle():
+            end(0)
+            begin(1)
+
+        self.start, self.finish = lambda: begin(0), finish
+        self.steps = [middle, lambda: end(1)]
+
+
+def exchange_kernel(jobs, *refs):
+    kinds = ([len(j.inputs) for j in jobs], [len(j.outputs) for j in jobs])
+    kinds += ([len(j.scratch) for j in jobs],)
+    at, cuts = 0, []
+    for lengths in kinds:
+        row = []
+        for length in lengths:
+            row.append(refs[at : at + length])
+            at += length
+        cuts.append(row)
+    peers = {}
+    for job, ins, outs, scratch in zip(jobs, *cuts):
+        job.bind(ins, outs, scratch)
+        peers.update(job.peers)
+    greet(list(peers.values()))
+    for job in jobs:
+        job.start()
+    for turn in range(max(len(job.steps) for job in jobs)):
+        for job in jobs:
+            if turn < len(job.steps):
+                job.steps[turn]()
+    for job in jobs:
+        job.finish()
+
+
+def exchange(jobs, ident):
+    def joined(field):
+        return [entry for job in jobs for entry in getattr(job, field)]
+
+    results = pl.pallas_call(
+        functools.partial(exchange_kernel, jobs),
+        out_shape=joined("outputs"),
+        in_specs=joined("in_specs"),
+        out_specs=joined("out_specs"),
+        scratch_shapes=joined("scratch"),
+        compiler_params=pltpu.CompilerParams(
+            collective_id=ident, has_side_effects=True, vmem_limit_bytes=VMEM_LIMIT
+        ),
+        name="exchange_" + str(ident),
+    )(*joined("inputs"))
+    cuts, at = [], 0
+    for job in jobs:
+        cuts.append(results[at : at + len(job.outputs)])
+        at += len(job.outputs)
+    return cuts
 
 
 def positions(start, rows, keys):
@@ -631,6 +722,15 @@
     return low, high
 
 
+def flat_rows(gathered):
+    return [a.reshape(a.shape[0] * a.shape[1], a.shape[2]) for a in gathered]
+
+
+def blocked(grad, shards):
+    rows, cols = grad.shape
+    return grad.astype(jnp.bfloat16).reshape(shards // 2, 2, rows // shards, cols)
+
+
 def product(left, right):
     return jnp.dot(left, right, preferred_element_type=jnp.float32)
 
@@ -700,28 +800,15 @@
     mask = (frame_pos[None, :] < lengths_flat[:, None]).astype(jnp.float32).reshape(rows, 1)
     mask_micro = mask.reshape(micro_count, seqs * local, 1)
 
-    whole_second_up = lax.all_gather(second_up, "fsdp", axis=0, tiled=True)
-    whole_second_down = lax.all_gather(second_down, "fsdp", axis=0, tiled=True)
     small = jnp.concatenate([depthwise, gains.T, batch_shift[:, None]], axis=1)
     small_cols = small.shape[1]
     small_width = 256
     small = jnp.pad(small, ((0, 0), (0, small_width - small_cols)))
-    gathered = gather(
-        [first_up, small, first_down, project_in, project_out, pointwise_in, pointwise_out],
-        "fsdp",
-        "ctx",
-        0,
-    )
-    gathered = [a.reshape(a.shape[0] * a.shape[1], a.shape[2]) for a in gathered]
-    (
-        whole_first_up,
-        whole_small,
-        whole_first_down,
-        whole_project_in,
-        whole_project_out,
-        whole_pointwise_in,
-        whole_pointwise_out,
-    ) = gathered
+    early = Gather(
+        [first_up, small, first_down, project_in], "fsdp", "ctx", (True, False, True, False)
+    )
+    (gathered,) = exchange([early], 0)
+    whole_first_up, whole_small, whole_first_down, whole_project_in = flat_rows(gathered)
     small_rows = whole_small[:, :small_cols].astype(jnp.float32).T
     tap_weights = jnp.pad(small_rows[:taps], ((0, tap_rows - taps), (0, 0)))
     gain_rows = small_rows[taps : taps + gain_count]
@@ -735,7 +822,10 @@
     normed_attend, unit_attend, inverse_attend = layer_norm(stream_first, gain_rows[1])
     triple = product(normed_attend, whole_project_in).astype(bf16)
     queries = triple[:, :width].reshape(batch, local, width)
-    (keyvals,) = gather([triple[:, width:].reshape(batch, local, 2 * width)], "ctx", None, 1)
+    keyvals = Gather([triple[:, width:].reshape(batch, local, 2 * width)], "ctx")
+    later = Gather([project_out, pointwise_in, pointwise_out, second_up], "fsdp", "ctx")
+    ((keyvals,), gathered) = exchange([keyvals, later], 1)
+    whole_project_out, whole_pointwise_in, whole_pointwise_out, whole_second_up = flat_rows(gathered)
     context = attend(start, lengths_flat, head_terms, queries, keyvals).reshape(rows, width)
     stream_attend = stream_first + product(context, whole_project_out)
     normed_conv, unit_conv, inverse_conv = layer_norm(stream_attend, gain_rows[2])
@@ -757,7 +847,10 @@
     )
     moment_rows = -(-moments.shape[0] // 8) * 8
     moments = jnp.pad(moments, ((0, moment_rows - moments.shape[0]), (0, 0)))
-    moments = channel_merge(moments, functools.partial(merge_moments, micro_count), 2)
+    merging = Channels(moments, functools.partial(merge_moments, micro_count))
+    last = Gather([second_down], "fsdp", "ctx", (True,))
+    ((moments,), gathered) = exchange([merging, last], 2)
+    (whole_second_down,) = flat_rows(gathered)
     count = moments[2 * micro_count : 3 * micro_count][:, None, :]
     bn_mean = moments[:micro_count][:, None, :] / count
     inverse_bn = lax.rsqrt(moments[micro_count : 2 * micro_count][:, None, :] / count + EPS)
@@ -783,24 +876,15 @@
     )
     grad_second_up = product_left(normed_second, dup_second)
     grad_second_down = product_left(act_second, dsecond_low)
-    second_pack = jnp.concatenate(
-        [
-            piece
-            for grad in (grad_second_up, grad_second_down)
-            for piece in jnp.split(
-                grad.astype(bf16).reshape(shards, -1, grad.shape[1]), grad.shape[1] // width, axis=2
-            )
-        ],
-        axis=1,
-    )
-    second_shard = lax.psum_scatter(second_pack, "fsdp", scatter_dimension=0, tiled=True)
-    second_sum = lax.psum(second_shard[0], "ctx")
-    up_rows = second_up.shape[0]
-    up_blocks = second_up.shape[1] // width
-    second_up_sum = jnp.concatenate(
-        [second_sum[i * up_rows : (i + 1) * up_rows] for i in range(up_blocks)], axis=1
-    ).astype(jnp.float32)
-    second_down_sum = second_sum[up_rows * up_blocks :].astype(jnp.float32)
+    second_parts = [
+        lax.psum_scatter(
+            grad.astype(bf16).reshape(shards, -1, grad.shape[1]),
+            "fsdp",
+            scatter_dimension=0,
+            tiled=True,
+        )[0]
+        for grad in (grad_second_down, grad_second_up)
+    ]
 
     dconv_stream = dsecond_stream + dtemp
     dconv_low = dconv_stream.astype(bf16)
@@ -812,7 +896,7 @@
     channel = jnp.concatenate([own_shift, own_cross], axis=0)
     channel_rows = -(-channel.shape[0] // 8) * 8
     channel = jnp.pad(channel, ((0, channel_rows - channel.shape[0]), (0, 0)))
-    channel = channel_merge(channel, merge_sums, 3)
+    ((channel,),) = exchange([Channels(channel, merge_sums)], 3)
     sum_shift = channel[:micro_count][:, None, :]
     sum_cross = channel[micro_count : 2 * micro_count][:, None, :]
     ddepth = (
@@ -837,7 +921,19 @@
     )
     splits = dkeyvals.shape[0] // 2
     dkeyvals = dkeyvals.reshape(splits, 2, rows, 2 * width)
-    (dkeyvals,) = scatter([dkeyvals], "ctx", None, bf16, 4)
+    conv_grads = [
+        product_left(normed_conv, dexpanded),
+        product_left(act_conv, dconv_low),
+        product_left(context, dattend_low),
+    ]
+    ((dkeyvals,), conv_sums) = exchange(
+        [
+            Scatter([dkeyvals], "ctx", None, bf16),
+            Scatter([blocked(g, shards) for g in conv_grads], "fsdp", "ctx", jnp.float32),
+        ],
+        4,
+    )
+    grad_pointwise_in, grad_pointwise_out, grad_project_out = conv_sums
     dtriple = jnp.concatenate([dquery.reshape(rows, width), dkeyvals], axis=1)
     dtemp, gain_attend = norm_back(
         product_right(dtriple, whole_project_in), unit_attend, inverse_attend, gain_rows[1]
@@ -870,23 +966,17 @@
         product_left(act_first, dfirst_low),
         product_left(normed_first, dup_first),
         product_left(normed_attend, dtriple),
-        product_left(normed_conv, dexpanded),
-        product_left(context, dattend_low),
-        product_left(act_conv, dconv_low),
         small_block,
     ]
-    blocks = [
-        g.astype(bf16).reshape(shards // 2, 2, g.shape[0] // shards, g.shape[1]) for g in grads
-    ]
-    (
-        grad_first_down,
-        grad_first_up,
-        grad_project_in,
-        grad_pointwise_in,
-        grad_project_out,
-        grad_pointwise_out,
-        small_sum,
-    ) = scatter(blocks, "fsdp", "ctx", jnp.float32, 5)
+    (second_sums, sums) = exchange(
+        [
+            Scatter(second_parts, None, "ctx", jnp.float32),
+            Scatter([blocked(g, shards) for g in grads], "fsdp", "ctx", jnp.float32),
+        ],
+        5,
+    )
+    second_down_sum, second_up_sum = second_sums
+    grad_first_down, grad_first_up, grad_project_in, small_sum = sums
     heads_at = small_width // 2
     return (
         output,

time: 415 us -> 396 us (0.954)
  waiting for transfers between devices: 34.6 us -> 20.6 us
  matrix products: 42.1 us -> 37.2 us
    psum x1 -> x0, waiting for transfers between devices: 32 us -> none  [per_device(): second_sum = lax.psum(second_shard[0], 'ctx')]
    reduce_scatter x1 -> x2, waiting for transfers between devices: 0.02 us -> 20 us  [per_device(): lax.psum_scatter(grad.astype(bf16).reshape(shards, -1, grad.shape[1]), 'f...]
    dot_general x8, matrix products: 14 us -> 8.82 us  [product(): return jnp.dot(left, right, preferred_element_type=jnp.float32)]
    unnamed x161 -> x159, local copies, waits for them, and re-layouts: 15.8 us -> 16.2 us
  transfers between devices with their start and end apart: 8 -> 6, of which waited for: 2 -> 2; matrix products, arithmetic and copies ran while one was open for 16% -> 10% of each run, Pallas kernels for 63% -> 21%
where the time goes in v2:
time: 396 us; the launch traced here: 393 us
  Pallas kernels  262 us (66%)
  matrix products  37.2 us (9%)
  local copies, waits for them, and re-layouts  25.8 us (7%)
  other arithmetic  24.3 us (6%)
  waiting for transfers between devices  20.6 us (5%)
  between operations  15 us (4%)
  starting transfers between devices  8.4 us (2%)
    pallas_call x6, Pallas kernels, exchange(): pl.pallas_call(functools.partial(exchange_kernel, jobs), out_shape=joined...  229 us
    reduce_scatter x2, waiting for transfers between devices, per_device(): lax.psum_scatter(grad.astype(bf16).reshape(shards, -1, grad.shape[1]), 'f...  20 us
    unnamed x159, local copies, waits for them, and re-layouts  16.2 us
    dot_general x8, matrix products, product_left(): return jnp.dot(left.T, right, preferred_element_type=jnp.float32)  14.3 us
    dot_general x8, matrix products, product_right(): return jnp.dot(left, right.T, preferred_element_type=jnp.float32)  14 us
    pallas_call x1, Pallas kernels, attend_back(): pl.pallas_call(attend_back_kernel, grid=(batch,), out_shape=[jax.ShapeDty...  13.2 us
    dot_general x8, matrix products, product(): return jnp.dot(left, right, preferred_element_type=jnp.float32)  8.82 us
    pallas_call x1, Pallas kernels, attend(): pl.pallas_call(attend_kernel, grid=(batch,), out_shape=jax.ShapeDtypeStru...  8.61 us
  transfers between devices with their start and end apart: 6, of which 2 were waited for; matrix products, arithmetic and copies ran while one was open for 10% of the time, Pallas kernels for 21%

profile of v2, /device:TPU:0, one launch (start us, length us, event | category | flops | bytes accessed | tf_op | source)
XLA Modules:
  0.0 393.5 jit_solution(1951709229226732096)
XLA Ops:
  13.7 40.0 %exchange_0.1 = (bf16[8,64,2048]{2,1,0:T(8,128)(2,1)}, bf16[8,64,256]{2,1,0:T(8,128)(2,1)}, bf16[8,256,512]{2,1,0:T(8,128)(2,1)}, bf16[8,64,1536]{2,1,0:T(8,128)(2,1)}) custom-call(bf16[64,2048]{1,0:T(8,128)(2,1)} %refs_0_.1, bf16[64,256]{1,0:T(8,128)(2,1)} %fusion.28.refs_1_, bf16[256,512]{1,0:T(8,128)(2,1)} %refs_2_.2, bf16[64,1536]{1,0:T(8,128)(2,1)} %refs_3_.2), custom_call_target="tpu_custom_call" | custom-call | tf_op jit(solution)/shard_map/exchange_0/pallas_call | solution.py:505
  55.0 2.4 fusion.53
  61.9 40.4 %exchange_1.1 = (bf16[4,2,128,1024]{3,2,1,0:T(8,128)(2,1)}, bf16[8,64,512]{2,1,0:T(8,128)(2,1)}, bf16[8,64,1024]{2,1,0:T(8,128)(2,1)}, bf16[8,64,512]{2,1,0:T(8,128)(2,1)}, bf16[8,64,2048]{2,1,0:T(8,128)(2,1)}) custom-call(bf16[2,128,1024]{2,1,0:T(8,128)(2,1)} %bitcast.155, bf16[64,512]{1,0:T(8,128)(2,1)} %refs_1_.2, bf16[64,1024]{1,0:T(8,128)(2,1)} %refs_2_.3, ...), custom_call_target="tpu_custom_call" | custom-call | tf_op jit(solution)/shard_map/exchange_1/pallas_call | solution.py:505
  102.3 8.6 %attend.1 = bf16[2,128,512]{2,1,0:T(8,128)(2,1)} custom-call(s32[1]{0:T(128)} %bitcast.9.start_ref, s32[2]{0:T(128)} %bitcast.206, f32[2,8]{1,0:T(2,128)} %terms_ref.3, bf16[2,128,512]{2,1,0:T(8,128)(2,1)} %bitcast.144, bf16[4,2,128,1024]{3,2,1,0:T(8,128)(2,1)} %get-tuple-element.44.kv_ref), custom_call_target="tpu_custom_call" | custom-call | tf_op jit(solution)/shard_map/attend/pallas_call | solution.py:604
  113.4 2.3 collective-permute-start
  119.6 5.0 %depth_apply.1 = f32[2,128,512]{2,1,0:T(8,128)} custom-call(bf16[2,160,512]{2,1,0:T(8,128)(2,1)} %pad_maximum_fusion.6.padded_ref, f32[32,512]{1,0:T(8,128)} %slice_select_fusion.weight_ref), custom_call_target="tpu_custom_call" | custom-call | tf_op jit(solution)/shard_map/depth_apply/pallas_call | solution.py:677
  127.7 24.6 %exchange_2.1 = (f32[8,512]{1,0:T(8,128)}, bf16[8,256,512]{2,1,0:T(8,128)(2,1)}) custom-call(f32[8,512]{1,0:T(8,128)} %pad.28.refs_0_, bf16[256,512]{1,0:T(8,128)(2,1)} %refs_1_.3), custom_call_target="tpu_custom_call" | custom-call | tf_op jit(solution)/shard_map/exchange_2/pallas_call | solution.py:505
  160.6 2.2 convolution_convert_fusion.3
  162.8 3.5 fusion
  169.1 1.9 fusion.20
  171.6 13.5 %exchange_3.1 = f32[8,512]{1,0:T(8,128)} custom-call(f32[8,512]{1,0:T(8,128)} %select_maximum_fusion.refs_0_), custom_call_target="tpu_custom_call" | custom-call | tf_op jit(solution)/shard_map/exchange_3/pallas_call | solution.py:505
  186.0 2.1 fusion.43
  189.4 3.3 collective-permute-start.2
  192.7 2.3 convolution_convert_fusion.2
  196.7 6.0 %depth_back.1 = (f32[2,128,512]{2,1,0:T(8,128)}, f32[2,32,512]{2,1,0:T(8,128)}) custom-call(bf16[2,160,512]{2,1,0:T(8,128)(2,1)} %pad_maximum_fusion.6.padded_ref, bf16[2,16,512]{2,1,0:T(8,128)(2,1)} %copy-done.39, bf16[2,16,512]{2,1,0:T(8,128)(2,1)} %copy-done.38, f32[2,128,512]{2,1,0:T(8,128)} %get-tuple-element.155.ddepth_ref, ...), custom_call_target="tpu_custom_call" | custom-call | tf_op jit(solution)/shard_map/depth_back/pallas_call | solution.py:693
  206.6 13.2 %attend_back.1 = (bf16[2,128,512]{2,1,0:T(8,128)(2,1)}, bf16[4,2,128,1024]{3,2,1,0:T(8,128)(2,1)}, f32[2,16,512]{2,1,0:T(8,128)}) custom-call(s32[1]{0:T(128)} %bitcast.9.start_ref, s32[2]{0:T(128)} %bitcast.207, f32[2,8]{1,0:T(2,128)} %terms_ref.3, bf16[2,128,512]{2,1,0:T(8,128)(2,1)} %bitcast.145, bf16[4,2,128,1024]{3,2,1,0:T(8,128)(2,1)} %get-tuple-element.44.kv_ref, ...), custom_call_target="tpu_custom_call" | custom-call | tf_op jit(solution)/shard_map/attend_back/pallas_call | solution.py:622
  224.1 50.6 %exchange_4.1 = (bf16[256,1024]{1,0:T(8,128)(2,1)}, f32[64,1024]{1,0:T(8,128)}, f32[64,512]{1,0:T(8,128)}, f32[64,512]{1,0:T(8,128)}) custom-call(bf16[2,2,256,1024]{3,2,1,0:T(8,128)(2,1)} %bitcast.154, bf16[4,2,64,1024]{3,2,1,0:T(8,128)(2,1)} %bitcast.141, bf16[4,2,64,512]{3,2,1,0:T(8,128)(2,1)} %bitcast.158, bf16[4,2,64,512]{3,2,1,0:T(8,128)(2,1)} %bitcast.159), custom_call_target="tpu_custom_call" | custom-call | tf_op jit(solution)/shard_map/exchange_4/pallas_call | solution.py:505
  274.7 2.5 multiply_reduce_fusion.2
  286.1 1.9 convolution_convert_fusion.4
  288.0 2.0 convolution_convert_fusion
  290.0 2.2 convolution_convert_fusion.1
  292.2 20.0 %reduce-scatter.5.cloned.1.call-done = bf16[1,64,2048]{2,1,0:T(8,128)(2,1)} async-done(((bf16[8,64,2048]{2,1,0:T(8,128)(2,1)}), bf16[1,64,2048]{2,1,0:T(8,128)(2,1)}) %reduce-scatter.5.cloned.1.call-update) | async-done | bytes 262160 | tf_op jit(solution)/shard_map/reduce_scatter | solution.py:880
  312.2 60.3 %exchange_5.1 = (f32[256,512]{1,0:T(8,128)}, f32[64,2048]{1,0:T(8,128)}, f32[256,512]{1,0:T(8,128)}, f32[64,2048]{1,0:T(8,128)}, f32[64,1536]{1,0:T(8,128)}, /*index=5*/f32[64,256]{1,0:T(8,128)}) custom-call(bf16[256,512]{1,0:T(8,128)(2,1)} %bitcast.173, bf16[64,2048]{1,0:T(8,128)(2,1)} %bitcast.174, bf16[4,2,256,512]{3,2,1,0:T(8,128)(2,1)} %bitcast.148, ...), custom_call_target="tpu_custom_call" | custom-call | tf_op jit(solution)/shard_map/exchange_5/pallas_call | solution.py:505
  380.3 1.9 copy.90
  (255 shorter events, 65.7 us)
Async XLA Ops:
  7.2 47.6 %copy-start.1 = (bf16[2,1,128,512]{3,2,1,0:T(8,128)(2,1)S(1)}, bf16[2,1,128,512]{3,2,1,0:T(8,128)(2,1)}, u32[]{:S(2)}) copy-start(bf16[2,1,128,512]{3,2,1,0:T(8,128)(2,1)} %param.15) | copy-start | bytes 786436
  7.2 285.0 %reduce-scatter.3.cloned.1.call-start = ((), (), s32[]{:S(2)}) async-start(), calls=%async_computation.2 | async-start | bytes 2359296 | tf_op jit(solution)/shard_map/reduce_scatter | solution.py:880
  54.8 150.4 %copy-start.40 = (f32[1,512]{1,0:T(1,128)}, f32[1,512]{1,0:T(1,128)S(1)}, u32[]{:S(2)}) copy-start(f32[1,512]{1,0:T(1,128)S(1)} %get-tuple-element.173) | copy-start | bytes 6148
  61.9 51.2 %copy-start.57 = (f32[256]{0:T(256)}, f32[256]{0:T(256)S(1)}, u32[]{:S(2)}) copy-start(f32[256]{0:T(256)S(1)} %get-tuple-element.185) | copy-start | bytes 3076
  113.4 4.9 %collective-permute-start = (bf16[2,16,512]{2,1,0:T(8,128)(2,1)S(1)}, bf16[2,16,512]{2,1,0:T(8,128)(2,1)S(1)}, u32[]{:S(2)}, u32[]{:S(2)}) collective-permute-start(bf16[2,16,512]{2,1,0:T(8,128)(2,1)S(1)} %get-tuple-element.167), channel_id=1, source_target_pairs={{0,1},{1,2},{2,3},{4,5},{5,6},{6,7},{8,9},{9,10},{10,11},{12,13},{... | collective-permute-start | bytes 98312 | tf_op jit(solution)/shard_map/ppermute | solution.py:720
  115.7 3.2 collective-permute-start.1
  162.8 149.4 %reduce-scatter.5.cloned.1.call-start = ((), (), s32[]{:S(2)}) async-start(), calls=%async_computation.3 | async-start | bytes 2359296 | tf_op jit(solution)/shard_map/reduce_scatter | solution.py:880
  188.1 8.0 %collective-permute-start.3 = (bf16[2,16,512]{2,1,0:T(8,128)(2,1)S(1)}, bf16[2,16,512]{2,1,0:T(8,128)(2,1)S(1)}, u32[]{:S(2)}, u32[]{:S(2)}) collective-permute-start(bf16[2,16,512]{2,1,0:T(8,128)(2,1)S(1)} %get-tuple-element.165), channel_id=1, source_target_pairs={{1,0},{2,1},{3,2},{5,4},{6,5},{7,6},{9,8},{10,9},{11,10},{13,12},{... | collective-permute-start | bytes 98312 | tf_op jit(solution)/shard_map/ppermute | solution.py:721
  189.4 6.7 %collective-permute-start.2 = (bf16[2,16,512]{2,1,0:T(8,128)(2,1)S(1)}, bf16[2,16,512]{2,1,0:T(8,128)(2,1)S(1)}, u32[]{:S(2)}, u32[]{:S(2)}) collective-permute-start(bf16[2,16,512]{2,1,0:T(8,128)(2,1)S(1)} %get-tuple-element.166), channel_id=1, source_target_pairs={{0,1},{1,2},{2,3},{4,5},{5,6},{6,7},{8,9},{9,10},{10,11},{12,13},{... | collective-permute-start | bytes 98312 | tf_op jit(solution)/shard_map/ppermute | solution.py:720
  205.5 15.2 %copy-start.35 = (f32[2,32,512]{2,1,0:T(8,128)S(1)}, f32[2,32,512]{2,1,0:T(8,128)}, u32[]{:S(2)}) copy-start(f32[2,32,512]{2,1,0:T(8,128)} %get-tuple-element.55) | copy-start | bytes 393220
  205.5 15.9 %copy-start.2 = (bf16[2,128,512]{2,1,0:T(8,128)(2,1)S(1)}, bf16[2,128,512]{2,1,0:T(8,128)(2,1)}, u32[]{:S(2)}) copy-start(bf16[2,128,512]{2,1,0:T(8,128)(2,1)} %attend.1) | copy-start | bytes 786436
  206.6 15.9 %copy-start.23 = (bf16[256,512]{1,0:T(8,128)(2,1)S(1)}, bf16[256,512]{1,0:T(8,128)(2,1)}, u32[]{:S(2)}) copy-start(bf16[256,512]{1,0:T(8,128)(2,1)} %copy-done.22) | copy-start | bytes 786436
  206.6 15.9 %copy-start.25 = (bf16[256,512]{1,0:T(8,128)(2,1)S(1)}, bf16[256,512]{1,0:T(8,128)(2,1)}, u32[]{:S(2)}) copy-start(bf16[256,512]{1,0:T(8,128)(2,1)} %copy-done.24) | copy-start | bytes 786436
  206.6 15.9 %copy-start.41 = (f32[1,512]{1,0:T(1,128)S(1)}, f32[1,512]{1,0:T(1,128)}, u32[]{:S(2)}) copy-start(f32[1,512]{1,0:T(1,128)} %copy-done.40) | copy-start | bytes 6148
  224.0 50.6 %copy-start.17 = (bf16[8,64,1536]{2,1,0:T(8,128)(2,1)S(1)}, bf16[8,64,1536]{2,1,0:T(8,128)(2,1)}, u32[]{:S(2)}) copy-start(bf16[8,64,1536]{2,1,0:T(8,128)(2,1)} %get-tuple-element.43) | copy-start | bytes 4718596
  224.0 50.6 %copy-start.33 = (bf16[2,128,512]{2,1,0:T(8,128)(2,1)S(1)}, bf16[2,128,512]{2,1,0:T(8,128)(2,1)}, u32[]{:S(2)}) copy-start(bf16[2,128,512]{2,1,0:T(8,128)(2,1)} %get-tuple-element.52) | copy-start | bytes 786436
  224.0 50.6 %copy-start.43 = (f32[1,512]{1,0:T(1,128)S(1)}, f32[1,512]{1,0:T(1,128)}, u32[]{:S(2)}) copy-start(f32[1,512]{1,0:T(1,128)} %copy-done.42) | copy-start | bytes 6148
  224.0 50.6 %copy-start.48 = (f32[256]{0:T(256)S(1)}, f32[256]{0:T(256)}, u32[]{:S(2)}) copy-start(f32[256]{0:T(256)} %copy-done.47) | copy-start | bytes 3076
  224.1 50.6 %copy-start.55 = (f32[256]{0:T(256)S(1)}, f32[256]{0:T(256)}, u32[]{:S(2)}) copy-start(f32[256]{0:T(256)} %copy-done.54) | copy-start | bytes 3076
  372.5 9.7 %copy-start.30 = (f32[64,1536]{1,0:T(8,128)S(1)}, f32[64,1536]{1,0:T(8,128)}, u32[]{:S(2)}) copy-start(f32[64,1536]{1,0:T(8,128)} %get-tuple-element.219) | copy-start | bytes 1179652
  372.5 10.5 %copy-start.37 = (f32[64,512]{1,0:T(8,128)S(1)}, f32[64,512]{1,0:T(8,128)}, u32[]{:S(2)}) copy-start(f32[64,512]{1,0:T(8,128)} %get-tuple-element.220) | copy-start | bytes 393220
  372.6 11.1 %copy-start.32 = (f32[64,1024]{1,0:T(8,128)S(1)}, f32[64,1024]{1,0:T(8,128)}, u32[]{:S(2)}) copy-start(f32[64,1024]{1,0:T(8,128)} %get-tuple-element.221) | copy-start | bytes 786436
  372.6 11.8 %copy-start.36 = (f32[64,512]{1,0:T(8,128)S(1)}, f32[64,512]{1,0:T(8,128)}, u32[]{:S(2)}) copy-start(f32[64,512]{1,0:T(8,128)} %get-tuple-element.223) | copy-start | bytes 393220
  373.4 11.7 %copy-start.28 = (f32[64,2048]{1,0:T(8,128)S(1)}, f32[64,2048]{1,0:T(8,128)}, u32[]{:S(2)}) copy-start(f32[64,2048]{1,0:T(8,128)} %get-tuple-element.224) | copy-start | bytes 1572868
  (55 other events, 166.6 us)
Sparse Core Ops, SparseCore 0:
  162.9 71.1 reduce-scatter.2
  237.6 74.5 reduce-scatter.4

commit v3 on v2

--- a/solution.py
+++ b/solution.py
@@ -48,7 +48,16 @@
     )
 
 
+UNROLL = 8
+PIECE, SUM_PIECE = 64 * 1024, 64 * 512
+
+
 def steps(first, last, body):
+    if last - first <= UNROLL:
+        for i in range(first, last):
+            body(i)
+        return
+
     def step(i, carry):
         body(i)
         return carry
@@ -60,337 +69,438 @@
     return pltpu.SemaphoreType.DMA(shape)
 
 
-def staged(count, stages):
+def pieces_of(array, shape, least, size):
+    rows, cols = shape
+    want = max(1, rows * cols // size)
+    across = max(k for k in range(1, want + 1) if cols % (least * k) == 0 or k == 1)
+    down = max(k for k in range(1, want // across + 1) if rows % (16 * k) == 0 or k == 1)
+    height, width = rows // down, cols // across
     return [
-        functools.partial(stage, step - index)
-        for step in range(count + len(stages) - 1)
+        (array, i * height, height, j * width, width) for i in range(down) for j in range(across)
+    ]
+
+
+def turns(index, count):
+    if count > UNROLL:
+        return lambda step: rotated(index, step, count)
+    known = {0: index}
+    for step in range(1, count):
+        known[step] = rotated(index, step, count)
+    return lambda step: known[step % count] if isinstance(step, int) else rotated(index, step, count)
+
+
+LAG, SUM_LAG = 2, 3
+AHEAD = 2
+
+
+def staged(count, stages, lag):
+    return [
+        functools.partial(stage, step - lag * index)
+        for step in range(count + lag * (len(stages) - 1))
         for index, stage in enumerate(stages)
-        if 0 <= step - index < count
+        if 0 <= step - lag * index < count
     ]
 
 
 class Gather:
     def __init__(self, arrays, axis, pair=None, shares=None):
         self.inputs, self.axis, self.pair = arrays, axis, pair
-        count, size = len(arrays), lax.axis_size(axis)
+        size = lax.axis_size(axis)
         places = 1 if pair is None else lax.axis_size(pair) // 2
         self.size, self.places = size, places
-        self.used = [places if shares and shares[a] else 1 for a in range(count)]
-        highs, most = size // 2, max(self.used)
-        self.in_specs = [VMEM] * count
-        self.out_specs = [ANY] * count
+        used = [places if shares and shares[a] else 1 for a in range(len(arrays))]
+        sides = 1 if pair is None else 2
+        self.pieces = [
+            piece
+            for a, array in enumerate(arrays)
+            for piece in pieces_of(a, array.shape, 128 * sides * used[a], PIECE)
+        ]
+        self.used = [used[piece[0]] for piece in self.pieces]
+        count, highs, most = len(self.pieces), size // 2, max(used)
+        self.in_specs = [VMEM] * len(arrays)
+        self.out_specs = [ANY] * len(arrays)
         self.outputs = [jax.ShapeDtypeStruct((size,) + a.shape, a.dtype) for a in arrays]
-        self.scratch = [dma(count)] + [dma(count, highs)] * 4
+        self.scratch = [dma(len(arrays))] + [dma(count, highs)] * 4
         if pair is not None:
-            self.scratch += [dma(count, size, most)] * 2
-            self.scratch += [dma(count, size, most)] * 2
+            self.scratch += [dma(count, size, most)] * 4
 
     def bind(self, ins, outs, scratch):
         axis, pair, size, places, used = self.axis, self.pair, self.size, self.places, self.used
-        count = len(ins)
+        pieces = self.pieces
+        count = len(pieces)
         keep, zs, zr, ys, yr = scratch[:5]
         me = lax.axis_index(axis)
         highs = size // 2
         low, high = lax.rem(me, 2), lax.div(me, 2)
-        partner = other_of(me)
-        self.peers = {(axis, d): {axis: 2 * rotated(high, d, highs) + low} for d in range(1, highs)}
+        partner, other = other_of(me), 1 - low
+        around, up = turns(me, size), turns(high, highs)
+        self.peers = {(axis, d): {axis: 2 * up(d) + low} for d in range(1, highs)}
         self.peers[axis, 0] = {axis: partner}
         if pair is not None:
             cs, cr, xs, xr = scratch[5:]
             spot = lax.axis_index(pair)
             side, place = lax.rem(spot, 2), lax.div(spot, 2)
+            beside = turns(place, places)
             pair_to = {pair: other_of(spot)}
             self.peers[pair, 0] = pair_to
             if max(used) > 1:
                 for e in range(1, places):
-                    self.peers[pair, e] = {pair: 2 * rotated(place, e, places) + side}
-
-        def part(a, ref, at=None, mine=True):
+                    self.peers[pair, e] = {pair: 2 * beside(e) + side}
+
+        def window(p, ref, at=None, mine=True):
+            _, row, rows, col, cols = pieces[p]
             if pair is None:
-                return ref
-            width = ref.shape[-1] // (2 * used[a])
+                return ref.at[pl.ds(row, rows), pl.ds(col, cols)]
+            width = cols // (2 * used[p])
             if at is None:
-                at = place if used[a] > 1 else 0
+                at = place if used[p] > 1 else 0
             index = 2 * at + (side if mine else 1 - side)
-            return ref.at[:, pl.ds(pl.multiple_of(index * width, width), width)]
-
-        def origin(d):
-            return 2 * rotated(high, -d, highs)
-
-        def along(a, d, landed=False):
-            spot_to = origin(d) + low if landed else me
+            start = pl.multiple_of(col + index * width, 128)
+            return ref.at[pl.ds(row, rows), pl.ds(start, width)]
+
+        def source(p):
+            return window(p, ins[pieces[p][0]])
+
+        def block(p, place, at=None, mine=True):
+            return window(p, outs[pieces[p][0]].at[place], at, mine)
+
+        def along(p, d, landed=False):
+            to = 2 * up(-d) + low if landed else me
             return send(
-                part(a, ins[a]),
-                part(a, outs[a].at[spot_to]),
-                zs.at[a, d],
-                zr.at[a, d],
-                {axis: 2 * rotated(high, d, highs) + low},
+                source(p), block(p, to), zs.at[p, d], zr.at[p, d], {axis: 2 * up(d) + low}
             )
 
-        def across_first(a, landed=False):
+        def across(p, d, landed=False):
+            from_ref = source(p) if isinstance(d, int) and d == 0 else block(p, 2 * up(-d) + low)
+            to = 2 * up(-d) + (other if landed else low)
+            return send(from_ref, block(p, to), ys.at[p, d], yr.at[p, d], {axis: partner})
+
+        def over(p, b, e, landed=False):
+            at = beside(-e) if landed else place
             return send(
-                part(a, ins[a]),
-                part(a, outs[a].at[partner if landed else me]),
-                ys.at[a, 0],
-                yr.at[a, 0],
-                {axis: partner},
+                block(p, b),
+                block(p, b, at),
+                xs.at[p, b, e],
+                xr.at[p, b, e],
+                {pair: 2 * beside(e) + side},
             )
 
-        def across(a, d, landed=False):
+        def hand(p, b, at, landed=False):
             return send(
-                part(a, outs[a].at[origin(d) + low]),
-                part(a, outs[a].at[origin(d) + (1 - low if landed else low)]),
-                ys.at[a, d],
-                yr.at[a, d],
-                {axis: partner},
-            )
-
-        def slot(a):
-            return place if used[a] > 1 else 0
-
-        def over(a, block, e, landed=False):
-            at = rotated(place, -e, places) if landed else place
-            return send(
-                part(a, outs[a].at[block]),
-                part(a, outs[a].at[block], at),
-                xs.at[a, block, e],
-                xr.at[a, block, e],
-                {pair: 2 * rotated(place, e, places) + side},
-            )
-
-        def hand(a, block, at, landed=False):
-            return send(
-                part(a, outs[a].at[block], at),
-                part(a, outs[a].at[block], at, not landed),
-                cs.at[a, block, at],
-                cr.at[a, block, at],
-                pair_to,
+                block(p, b, at), block(p, b, at, not landed), cs.at[p, b, at], cr.at[p, b, at], pair_to
             )
 
         def local(a):
             return pltpu.make_async_copy(ins[a], outs[a].at[me], keep.at[a])
 
-        def spread(a, block):
+        def spread(p, b):
             if pair is not None:
-                for e in range(1, used[a]):
-                    over(a, block, e).start()
-                hand(a, block, slot(a)).start()
+                for e in range(1, used[p]):
+                    over(p, b, e).start()
+                hand(p, b, place if used[p] > 1 else 0).start()
+
+        def begin(p):
+            if p < count:
+                steps(1, highs, lambda d: along(p, d).start())
+                across(p, 0).start()
 
         def start():
-            for a in range(count):
-                steps(1, highs, lambda d: along(a, d).start())
-                across_first(a).start()
-            for a in range(count):
+            for p in range(AHEAD):
+                begin(p)
+            for a in range(len(ins)):
                 local(a).start()
 
-        def first(a):
+        def first(p):
+            begin(p + AHEAD)
+
             def one(d):
-                along(a, d, True).wait_recv()
-                across(a, d).start()
-                spread(a, origin(d) + low)
+                along(p, d, True).wait_recv()
+                across(p, d).start()
+                spread(p, 2 * up(-d) + low)
 
             steps(1, highs, one)
 
-        def second(a):
-            across_first(a, True).wait_recv()
-            spread(a, partner)
-
+        def second(p):
             def one(d):
-                across(a, d, True).wait_recv()
-                spread(a, origin(d) + 1 - low)
-
+                across(p, d, True).wait_recv()
+                spread(p, 2 * up(-d) + other)
+
+            one(0)
             steps(1, highs, one)
 
-        def third(a):
-            for e in range(1, used[a]):
+        def third(p):
+            for e in range(1, used[p]):
 
                 def one(i):
-                    block = rotated(me, i, size)
-                    over(a, block, e, True).wait_recv()
-                    hand(a, block, rotated(place, -e, places)).start()
+                    over(p, around(i), e, True).wait_recv()
+                    hand(p, around(i), beside(-e)).start()
 
                 steps(1, size, one)
 
         def finish():
-            for a in range(count):
+            for p in range(count):
                 if pair is not None:
-                    for e in range(used[a]):
-                        at = rotated(place, -e, places) if used[a] > 1 else 0
-                        steps(1, size, lambda i: hand(a, rotated(me, i, size), at, True).wait_recv())
-                        steps(1, size, lambda i: hand(a, rotated(me, i, size), at).wait_send())
+                    for e in range(used[p]):
+                        at = beside(-e) if used[p] > 1 else 0
+                        steps(1, size, lambda i: hand(p, around(i), at, True).wait_recv())
+                        steps(1, size, lambda i: hand(p, around(i), at).wait_send())
                         if e > 0:
-                            steps(1, size, lambda i: over(a, rotated(me, i, size), e).wait_send())
-                steps(1, highs, lambda d: along(a, d).wait_send())
-                across_first(a).wait_send()
-                steps(1, highs, lambda d: across(a, d).wait_send())
+                            steps(1, size, lambda i: over(p, around(i), e).wait_send())
+                steps(1, highs, lambda d: along(p, d).wait_send())
+                across(p, 0).wait_send()
+                steps(1, highs, lambda d: across(p, d).wait_send())
+            for a in range(len(ins)):
                 local(a).wait()
 
         self.start, self.finish = start, finish
-        self.steps = staged(count, [first, second, third] if max(used) > 1 else [first, second])
+        self.steps = staged(
+            count, [first, second, third] if max(used) > 1 else [first, second], LAG
+        )
 
 
 class Scatter:
-    def __init__(self, arrays, axis, pair, dtype):
+    def __init__(self, arrays, axis, pair, dtype, shares=None):
         self.inputs, self.axis, self.pair = arrays, axis, pair
-        count = len(arrays)
-        self.size = 1 if axis is None else lax.axis_size(axis)
+        self.size = lax.axis_size(axis)
         self.pair_size = 1 if pair is None else lax.axis_size(pair)
         highs, places = self.size // 2, self.pair_size // 2
-        split = 1 if pair is None else 2
+        sides = 1 if pair is None else 2
+        used = [places if shares and shares[a] else 1 for a in range(len(arrays))]
         low_type = jnp.bfloat16
-        tail = [(a.shape[-2], a.shape[-1] // split) for a in arrays]
-        self.in_specs = [VMEM] * count
-        self.out_specs = [VMEM] * count
-        self.outputs = [jax.ShapeDtypeStruct(a.shape[-2:], dtype) for a in arrays]
-        self.scratch = []
+        self.pieces = [
+            piece
+            for a, array in enumerate(arrays)
+            for piece in pieces_of(a, array.shape[2:], 128 * sides * used[a], SUM_PIECE)
+        ]
+        self.used = [used[piece[0]] for piece in self.pieces]
+        count = len(self.pieces)
+        tail = [
+            (rows, cols // (sides * u)) for (_, _, rows, _, cols), u in zip(self.pieces, self.used)
+        ]
+        self.in_specs = [VMEM] * len(arrays)
+        self.out_specs = [VMEM] * len(arrays)
+        self.outputs = [jax.ShapeDtypeStruct(a.shape[2:], dtype) for a in arrays]
+        self.scratch = [pltpu.VMEM((highs,) + t, low_type) for t in tail]
+        self.scratch += [pltpu.VMEM((highs - 1,) + t, low_type) for t in tail]
+        self.scratch += [dma(count)] * 2 + [dma(count, highs)] * 2
         if pair is not None:
-            leads = () if axis is None else (highs, 2)
-            self.scratch += [pltpu.VMEM(leads + t, low_type) for t in tail]
-            self.scratch += [pltpu.VMEM((places,) + t, low_type) for t in tail]
-            self.scratch += [dma(count)] * 2 + [dma(count, places)] * 2 + [dma(count)] * 2
-        if axis is not None:
-            self.scratch += [pltpu.VMEM((highs,) + t, low_type) for t in tail]
-            self.scratch += [pltpu.VMEM((highs - 1,) + t, low_type) for t in tail]
-            self.scratch += [dma(count)] * 2 + [dma(count, highs)] * 2
+            wide = [(highs, 2, rows, cols * u) for (rows, cols), u in zip(tail, self.used)]
+            cut = [
+                (places - 1, highs, 2) + t if u > 1 else (1, 1, 1, 8, 128)
+                for t, u in zip(tail, self.used)
+            ]
+            cross = [(1, 8, 128) if u > 1 else (places,) + t for t, u in zip(tail, self.used)]
+            self.scratch += [pltpu.VMEM(t, low_type) for t in wide]
+            self.scratch += [pltpu.VMEM(t, low_type) for t in cut]
+            self.scratch += [pltpu.VMEM(t, low_type) for t in cross]
+            self.scratch += [dma(count)] * 2 + [dma(count, places)] * 6
 
     def bind(self, ins, outs, scratch):
         axis, pair, size, places = self.axis, self.pair, self.size, self.pair_size // 2
-        count = len(ins)
-        self.peers = {}
-        halves = ins
+        pieces, used = self.pieces, self.used
+        count = len(pieces)
+        lows, highs_in = scratch[:count], scratch[count : 2 * count]
+        ys, yr, zs, zr = scratch[2 * count : 2 * count + 4]
+        scratch = scratch[2 * count + 4 :]
+        me = lax.axis_index(axis)
+        highs = size // 2
+        low, high = lax.rem(me, 2), lax.div(me, 2)
+        up = turns(high, highs)
+        partner = {axis: other_of(me)}
+        self.peers = {(axis, d): {axis: 2 * up(d) + low} for d in range(1, highs)}
+        self.peers[axis, 0] = partner
         if pair is not None:
-            halves, cross = scratch[:count], scratch[count : 2 * count]
-            cs, cr, xs, xr, fs, fr = scratch[2 * count : 2 * count + 6]
-            scratch = scratch[2 * count + 6 :]
+            halves, cuts, cross = (scratch[i * count : (i + 1) * count] for i in range(3))
+            cs, cr, xs, xr, qs, qr, fs, fr = scratch[3 * count :]
             spot = lax.axis_index(pair)
             side, place = lax.rem(spot, 2), lax.div(spot, 2)
+            beside = turns(place, places)
             pair_to = {pair: other_of(spot)}
             self.peers[pair, 0] = pair_to
             for e in range(1, places):
-                self.peers[pair, e] = {pair: 2 * rotated(place, e, places) + side}
-        if axis is not None:
-            lows, highs_in = scratch[:count], scratch[count : 2 * count]
-            ys, yr, zs, zr = scratch[2 * count :]
-            me = lax.axis_index(axis)
-            highs = size // 2
-            low, high = lax.rem(me, 2), lax.div(me, 2)
-            partner = {axis: other_of(me)}
-            for d in range(1, highs):
-                self.peers[axis, d] = {axis: 2 * rotated(high, d, highs) + low}
-            self.peers[axis, 0] = partner
-
-        def columns(a, mine):
-            width = halves[a].shape[-1]
-            return pl.ds(pl.multiple_of((side if mine else 1 - side) * width, width), width)
-
-        def first(a):
-            theirs = columns(a, False)
-            piece = ins[a].at[:, theirs] if axis is None else ins[a].at[:, :, :, theirs]
-            return send(piece, halves[a], cs.at[a], cr.at[a], pair_to)
-
-        def across(a):
-            return send(halves[a].at[:, 1 - low], lows[a], ys.at[a], yr.at[a], partner)
-
-        def along(a, d):
-            to = rotated(high, d, highs)
+                self.peers[pair, e] = {pair: 2 * beside(e) + side}
+
+        def wide(value):
+            return value.astype(jnp.float32)
+
+        def each(last, body):
+            def step(i, carry):
+                body(i)
+                return carry
+
+            lax.fori_loop(0, last, step, 0)
+
+        def window(p, mine=True, at=None):
+            _, row, rows, col, cols = pieces[p]
+            if pair is None:
+                return pl.ds(row, rows), pl.ds(col, cols)
+            width = cols // (2 * used[p])
+            index = (side if mine else 1 - side) * used[p]
+            if used[p] > 1:
+                index = index + (place if at is None else at)
+            return pl.ds(row, rows), pl.ds(pl.multiple_of(col + index * width, 128), width)
+
+        def half(p, mine=True):
+            _, row, rows, col, cols = pieces[p]
+            start = pl.multiple_of(col + (side if mine else 1 - side) * (cols // 2), 128)
+            return pl.ds(row, rows), pl.ds(start, cols // 2)
+
+        def share(p, at):
+            width = pieces[p][4] // (2 * used[p])
+            return pl.ds(pl.multiple_of(at * width, 128), width)
+
+        def first(p):
+            rows, cols = half(p, False)
+            piece = ins[pieces[p][0]].at[:, :, rows, cols]
+            return send(piece, halves[p], cs.at[p], cr.at[p], pair_to)
+
+        def apart(p, e):
             return send(
-                lows[a].at[to],
-                highs_in[a].at[d - 1],
-                zs.at[a, d - 1],
-                zr.at[a, d - 1],
-                {axis: 2 * to + low},
+                halves[p].at[:, :, :, share(p, beside(e))],
+                cuts[p].at[e - 1],
+                qs.at[p, e],
+                qr.at[p, e],
+                {pair: 2 * beside(e) + side},
             )
 
-        def over(a, e, landed=False):
-            slot = rotated(place, -e, places) if landed else place
+        def across(p):
+            if pair is None:
+                rows, cols = window(p)
+                piece = ins[pieces[p][0]].at[:, 1 - low, rows, cols]
+            elif used[p] > 1:
+                piece = cuts[p].at[0, :, 1 - low]
+            else:
+                piece = halves[p].at[:, 1 - low]
+            return send(piece, lows[p], ys.at[p], yr.at[p], partner)
+
+        def along(p, d):
             return send(
-                cross[a].at[place],
-                cross[a].at[slot],
-                xs.at[a, e - 1],
-                xr.at[a, e - 1],
-                {pair: 2 * rotated(place, e, places) + side},
+                lows[p].at[up(d)],
+                highs_in[p].at[d - 1],
+                zs.at[p, d - 1],
+                zr.at[p, d - 1],
+                {axis: 2 * up(d) + low},
             )
 
-        def final(a, landed=False):
+        def over(p, e, landed=False):
+            slot = beside(-e) if landed else place
+            if used[p] > 1:
+                out = outs[pieces[p][0]]
+                source, target = out.at[window(p)], out.at[window(p, at=slot)]
+            else:
+                source, target = cross[p].at[place], cross[p].at[slot]
+            return send(source, target, xs.at[p, e], xr.at[p, e], {pair: 2 * beside(e) + side})
+
+        def final(p, e=0, landed=False):
+            out, at = outs[pieces[p][0]], beside(-e)
             return send(
-                outs[a].at[:, columns(a, True)],
-                outs[a].at[:, columns(a, not landed)],
-                fs.at[a],
-                fr.at[a],
+                out.at[window(p, at=at)],
+                out.at[window(p, not landed, at)],
+                fs.at[p, e],
+                fr.at[p, e],
                 pair_to,
             )
 
-        def wide(value):
-            return value.astype(jnp.float32)
-
-        def stage_first(a):
-            first(a).wait_recv()
-            if axis is None:
-                total = wide(ins[a][:, columns(a, True)]) + wide(halves[a][...])
-                cross[a][place] = total.astype(jnp.bfloat16)
-                for e in range(1, places):
-                    over(a, e).start()
-                return
+        def stage_first(p):
+            first(p).wait_recv()
+            rows, cols = half(p)
 
             def one(i):
                 for j in range(2):
-                    own = wide(ins[a][i, j, :, columns(a, True)])
-                    halves[a][i, j] = (own + wide(halves[a][i, j])).astype(jnp.bfloat16)
-
-            steps(0, highs, one)
-            across(a).start()
-
-        def stage_across(a):
-            across(a).wait_recv()
+                    own = wide(ins[pieces[p][0]][i, j, rows, cols])
+                    halves[p][i, j] = (own + wide(halves[p][i, j])).astype(jnp.bfloat16)
+
+            each(highs, one)
+            if used[p] > 1:
+                for e in range(1, places):
+                    apart(p, e).start()
+            else:
+                across(p).start()
+
+        def stage_apart(p):
+            if used[p] == 1:
+                return
+            for e in range(1, places):
+                apart(p, e).wait_recv()
 
             def one(i):
-                lows[a][i] = (wide(halves[a][i, low]) + wide(lows[a][i])).astype(jnp.bfloat16)
-
-            steps(0, highs, one)
-            steps(1, highs, lambda d: along(a, d).start())
-
-        def stage_along(a):
-            steps(1, highs, lambda d: along(a, d).wait_recv())
+                for j in range(2):
+                    total = wide(halves[p][i, j, :, share(p, place)])
+                    for e in range(1, places):
+                        total = total + wide(cuts[p][e - 1, i, j])
+                    cuts[p][0, i, j] = total.astype(jnp.bfloat16)
+
+            each(highs, one)
+            across(p).start()
+
+        def stage_across(p):
+            across(p).wait_recv()
+            rows, cols = window(p)
+
+            def one(i):
+                if pair is None:
+                    own = ins[pieces[p][0]][i, low, rows, cols]
+                else:
+                    own = cuts[p][0, i, low] if used[p] > 1 else halves[p][i, low]
+                lows[p][i] = (wide(own) + wide(lows[p][i])).astype(jnp.bfloat16)
+
+            each(highs, one)
+            steps(1, highs, lambda d: along(p, d).start())
+
+        def stage_along(p):
+            steps(1, highs, lambda d: along(p, d).wait_recv())
 
             def added(d, total):
-                return total + wide(highs_in[a][d - 1])
-
-            total = lax.fori_loop(1, highs, added, wide(lows[a][high]))
+                return total + wide(highs_in[p][d - 1])
+
+            total = lax.fori_loop(1, highs, added, wide(lows[p][high]))
+            out = outs[pieces[p][0]]
             if pair is None:
-                outs[a][...] = total.astype(outs[a].dtype)
+                out[window(p)] = total.astype(out.dtype)
                 return
-            cross[a][place] = total.astype(jnp.bfloat16)
+            if used[p] > 1:
+                out[window(p)] = total
+                final(p).start()
+            else:
+                cross[p][place] = total.astype(jnp.bfloat16)
             for e in range(1, places):
-                over(a, e).start()
-
-        def stage_over(a):
+                over(p, e).start()
+
+        def stage_over(p):
             for e in range(1, places):
-                over(a, e, True).wait_recv()
-            total = wide(cross[a][0])
-            for i in range(1, places):
-                total = total + wide(cross[a][i])
-            outs[a][:, columns(a, True)] = total
-            final(a).start()
+                over(p, e, True).wait_recv()
+                if used[p] > 1:
+                    final(p, e).start()
+            if used[p] == 1:
+                total = wide(cross[p][0])
+                for i in range(1, places):
+                    total = total + wide(cross[p][i])
+                outs[pieces[p][0]][window(p)] = total
+                final(p).start()
 
         def start():
-            for a in range(count):
-                (across(a) if pair is None else first(a)).start()
+            for p in range(count):
+                (across(p) if pair is None else first(p)).start()
 
         def finish():
-            for a in range(count):
-                if axis is not None:
-                    across(a).wait_send()
-                    steps(1, highs, lambda d: along(a, d).wait_send())
+            for p in range(count):
+                across(p).wait_send()
+                steps(1, highs, lambda d: along(p, d).wait_send())
                 if pair is not None:
-                    first(a).wait_send()
+                    first(p).wait_send()
                     for e in range(1, places):
-                        over(a, e).wait_send()
-                    final(a, True).wait_recv()
-                    final(a).wait_send()
-
-        middle = [] if axis is None else [stage_across, stage_along]
+                        over(p, e).wait_send()
+                        if used[p] > 1:
+                            apart(p, e).wait_send()
+                    for e in range(used[p]):
+                        final(p, e, True).wait_recv()
+                        final(p, e).wait_send()
+
+        middle = [stage_across, stage_along]
+        if max(used) > 1:
+            middle = [stage_apart] + middle
         stages = middle if pair is None else [stage_first] + middle + [stage_over]
-        self.start, self.finish, self.steps = start, finish, staged(count, stages)
+        self.start, self.finish, self.steps = start, finish, staged(count, stages, SUM_LAG)
 
 
 def merge_sums(parts):
@@ -713,6 +823,35 @@
     )(padded, dlow, dhigh, ddepth, weights)
 
 
+def results_kernel(count, taps, gains, heads_at, *refs):
+    ins, small, outs = refs[:count], refs[count], refs[count + 1 : 2 * count + 1]
+    depthwise, gain_rows, shift, heads, sems = refs[2 * count + 1 :]
+    copies = [pltpu.make_async_copy(ins[i], outs[i], sems.at[i]) for i in range(count)]
+    for copy in copies:
+        copy.start()
+    turned = small[:, :128].T
+    depthwise[...] = small[:, :taps]
+    gain_rows[...] = turned[taps : taps + gains]
+    shift[...] = turned[taps + gains : taps + gains + 1]
+    heads[...] = small[0:1, heads_at : heads_at + 2 * H]
+    for copy in copies:
+        copy.wait()
+
+
+def results(sums, small, taps, gains, heads_at):
+    rows, count = small.shape[0], len(sums)
+    shapes = [a.shape for a in sums] + [(rows, taps), (gains, rows), (1, rows), (1, 2 * H)]
+    return pl.pallas_call(
+        functools.partial(results_kernel, count, taps, gains, heads_at),
+        out_shape=[jax.ShapeDtypeStruct(shape, jnp.float32) for shape in shapes],
+        in_specs=[VMEM] * (count + 1),
+        out_specs=[ANY] * count + [VMEM] * 4,
+        scratch_shapes=[dma(count)],
+        compiler_params=pltpu.CompilerParams(vmem_limit_bytes=VMEM_LIMIT),
+        name="results",
+    )(*sums, small)
+
+
 def edges(block, width):
     count = lax.axis_size("ctx")
     forward = [(i, i + 1) for i in range(count - 1)]
@@ -822,10 +961,11 @@
     normed_attend, unit_attend, inverse_attend = layer_norm(stream_first, gain_rows[1])
     triple = product(normed_attend, whole_project_in).astype(bf16)
     queries = triple[:, :width].reshape(batch, local, width)
-    keyvals = Gather([triple[:, width:].reshape(batch, local, 2 * width)], "ctx")
+    keyvals = Gather([triple[:, width:]], "ctx")
     later = Gather([project_out, pointwise_in, pointwise_out, second_up], "fsdp", "ctx")
     ((keyvals,), gathered) = exchange([keyvals, later], 1)
     whole_project_out, whole_pointwise_in, whole_pointwise_out, whole_second_up = flat_rows(gathered)
+    keyvals = keyvals.reshape(keyvals.shape[0], batch, local, 2 * width)
     context = attend(start, lengths_flat, head_terms, queries, keyvals).reshape(rows, width)
     stream_attend = stream_first + product(context, whole_project_out)
     normed_conv, unit_conv, inverse_conv = layer_norm(stream_attend, gain_rows[2])
@@ -876,16 +1016,6 @@
     )
     grad_second_up = product_left(normed_second, dup_second)
     grad_second_down = product_left(act_second, dsecond_low)
-    second_parts = [
-        lax.psum_scatter(
-            grad.astype(bf16).reshape(shards, -1, grad.shape[1]),
-            "fsdp",
-            scatter_dimension=0,
-            tiled=True,
-        )[0]
-        for grad in (grad_second_down, grad_second_up)
-    ]
-
     dconv_stream = dsecond_stream + dtemp
     dconv_low = dconv_stream.astype(bf16)
     dshift = product_right(dconv_low, whole_pointwise_out).reshape(depth.shape) * swish_slope(
@@ -925,6 +1055,8 @@
         product_left(normed_conv, dexpanded),
         product_left(act_conv, dconv_low),
         product_left(context, dattend_low),
+        grad_second_down,
+        grad_second_up,
     ]
     ((dkeyvals,), conv_sums) = exchange(
         [
@@ -933,7 +1065,13 @@
         ],
         4,
     )
-    grad_pointwise_in, grad_pointwise_out, grad_project_out = conv_sums
+    (
+        grad_pointwise_in,
+        grad_pointwise_out,
+        grad_project_out,
+        grad_second_down,
+        grad_second_up,
+    ) = conv_sums
     dtriple = jnp.concatenate([dquery.reshape(rows, width), dkeyvals], axis=1)
     dtemp, gain_attend = norm_back(
         product_right(dtriple, whole_project_in), unit_attend, inverse_attend, gain_rows[1]
@@ -968,16 +1106,39 @@
         product_left(normed_attend, dtriple),
         small_block,
     ]
-    (second_sums, sums) = exchange(
+    (sums,) = exchange(
+        [Scatter([blocked(g, shards) for g in grads], "fsdp", "ctx", jnp.float32)], 5
+    )
+    grad_first_down, grad_first_up, grad_project_in, small_sum = sums
+    (
+        grad_first_up,
+        grad_first_down,
+        grad_project_in,
+        grad_project_out,
+        grad_pointwise_in,
+        grad_pointwise_out,
+        grad_second_up,
+        grad_second_down,
+        grad_depthwise,
+        grad_gains,
+        grad_shift,
+        grad_heads,
+    ) = results(
         [
-            Scatter(second_parts, None, "ctx", jnp.float32),
-            Scatter([blocked(g, shards) for g in grads], "fsdp", "ctx", jnp.float32),
+            grad_first_up,
+            grad_first_down,
+            grad_project_in,
+            grad_project_out,
+            grad_pointwise_in,
+            grad_pointwise_out,
+            grad_second_up,
+            grad_second_down,
         ],
-        5,
-    )
-    second_down_sum, second_up_sum = second_sums
-    grad_first_down, grad_first_up, grad_project_in, small_sum = sums
-    heads_at = small_width // 2
+        small_sum,
+        taps,
+        gain_count,
+        small_width // 2,
+    )
     return (
         output,
         grad_tokens,
@@ -986,13 +1147,13 @@
         grad_project_in,
         grad_project_out,
         grad_pointwise_in,
-        small_sum[:, :taps],
+        grad_depthwise,
         grad_pointwise_out,
-        second_up_sum,
-        second_down_sum,
-        small_sum[:, taps : taps + gain_count].T,
-        small_sum[:, taps + gain_count],
-        small_sum[0, heads_at : heads_at + 2 * H].reshape(2, H),
+        grad_second_up,
+        grad_second_down,
+        grad_gains,
+        grad_shift.reshape(batch_shift.shape),
+        grad_heads.reshape(head_terms.shape),
     )
 
 

time: 396 us -> 344 us (0.87)
  waiting for transfers between devices: 20.6 us -> 0.94 us
  between operations: 15 us -> 1.2 us
  local copies, waits for them, and re-layouts: 25.8 us -> 13.6 us
  matrix products: 37.2 us -> 31.9 us
  Pallas kernels: 262 us -> 266 us
    reduce_scatter x2 -> x0, waiting for transfers between devices: 20 us -> none  [per_device(): lax.psum_scatter(grad.astype(bf16).reshape(shards, -1, grad.shape[1]), 'f...]
    unnamed x159 -> x56, local copies, waits for them, and re-layouts: 16.2 us -> 7.43 us
    dot_general x8, matrix products: 14 us -> 8.79 us  [product_right(): return jnp.dot(left, right.T, preferred_element_type=jnp.float32)]
    pallas_call x0 -> x1, Pallas kernels: none -> 4.13 us  [results(): pl.pallas_call(functools.partial(results_kernel, count, taps, gains, head...]
  transfers between devices with their start and end apart: 6 -> 4, of which waited for: 2 -> 1; matrix products, arithmetic and copies ran while one was open for 10% -> 1% of each run, Pallas kernels for 21% -> 0%
where the time goes in v3:
time: 344 us; the launch traced here: 342 us
  Pallas kernels  266 us (77%)
  matrix products  31.9 us (9%)
  other arithmetic  20.5 us (6%)
  local copies, waits for them, and re-layouts  13.6 us (4%)
  starting transfers between devices  7.3 us (2%)
    pallas_call x6, Pallas kernels, exchange(): pl.pallas_call(functools.partial(exchange_kernel, jobs), out_shape=joined...  229 us
    dot_general x8, matrix products, product_left(): return jnp.dot(left.T, right, preferred_element_type=jnp.float32)  14.3 us
    pallas_call x1, Pallas kernels, attend_back(): pl.pallas_call(attend_back_kernel, grid=(batch,), out_shape=[jax.ShapeDty...  13.1 us
    dot_general x8, matrix products, product(): return jnp.dot(left, right, preferred_element_type=jnp.float32)  8.82 us
    dot_general x8, matrix products, product_right(): return jnp.dot(left, right.T, preferred_element_type=jnp.float32)  8.79 us
    pallas_call x1, Pallas kernels, attend(): pl.pallas_call(attend_kernel, grid=(batch,), out_shape=jax.ShapeDtypeStru...  8.6 us
    unnamed x56, local copies, waits for them, and re-layouts  7.43 us
  transfers between devices with their start and end apart: 4, of which 1 were waited for; matrix products, arithmetic and copies ran while one was open for 1% of the time, Pallas kernels for 0%

profile of v3, /device:TPU:0, one launch (start us, length us, event | category | flops | bytes accessed | tf_op | source)
XLA Modules:
  0.0 341.7 jit_solution(3817446279901807460)
XLA Ops:
  3.8 40.1 %exchange_0.1 = (bf16[8,64,2048]{2,1,0:T(8,128)(2,1)}, bf16[8,64,256]{2,1,0:T(8,128)(2,1)}, bf16[8,256,512]{2,1,0:T(8,128)(2,1)}, bf16[8,64,1536]{2,1,0:T(8,128)(2,1)}) custom-call(bf16[64,2048]{1,0:T(8,128)(2,1)} %refs_0_.1, bf16[64,256]{1,0:T(8,128)(2,1)} %fusion.28.refs_1_, bf16[256,512]{1,0:T(8,128)(2,1)} %refs_2_.2, bf16[64,1536]{1,0:T(8,128)(2,1)} %refs_3_.2), custom_call_target="tpu_custom_call" | custom-call | tf_op jit(solution)/shard_map/exchange_0/pallas_call | solution.py:615
  47.3 2.4 fusion.53
  54.2 37.9 %exchange_1.1 = (bf16[4,256,1024]{2,1,0:T(8,128)(2,1)}, bf16[8,64,512]{2,1,0:T(8,128)(2,1)}, bf16[8,64,1024]{2,1,0:T(8,128)(2,1)}, bf16[8,64,512]{2,1,0:T(8,128)(2,1)}, bf16[8,64,2048]{2,1,0:T(8,128)(2,1)}) custom-call(bf16[256,1024]{1,0:T(8,128)(2,1)} %slice.110.refs_0_, bf16[64,512]{1,0:T(8,128)(2,1)} %refs_1_.2, bf16[64,1024]{1,0:T(8,128)(2,1)} %refs_2_.3, ...), custom_call_target="tpu_custom_call" | custom-call | tf_op jit(solution)/shard_map/exchange_1/pallas_call | solution.py:615
  92.1 8.6 %attend.1 = bf16[2,128,512]{2,1,0:T(8,128)(2,1)} custom-call(s32[1]{0:T(128)} %bitcast.9.start_ref, s32[2]{0:T(128)} %bitcast.202, f32[2,8]{1,0:T(2,128)} %terms_ref.3, bf16[2,128,512]{2,1,0:T(8,128)(2,1)} %bitcast.143, bf16[4,2,128,1024]{3,2,1,0:T(8,128)(2,1)} %bitcast.135), custom_call_target="tpu_custom_call" | custom-call | tf_op jit(solution)/shard_map/attend/pallas_call | solution.py:714
  104.5 3.2 collective-permute-start
  109.6 5.0 %depth_apply.1 = f32[2,128,512]{2,1,0:T(8,128)} custom-call(bf16[2,160,512]{2,1,0:T(8,128)(2,1)} %pad_maximum_fusion.6.padded_ref, f32[32,512]{1,0:T(8,128)} %slice_select_fusion.weight_ref), custom_call_target="tpu_custom_call" | custom-call | tf_op jit(solution)/shard_map/depth_apply/pallas_call | solution.py:787
  117.7 26.5 %exchange_2.1 = (f32[8,512]{1,0:T(8,128)}, bf16[8,256,512]{2,1,0:T(8,128)(2,1)}) custom-call(f32[8,512]{1,0:T(8,128)} %pad.28.refs_0_, bf16[256,512]{1,0:T(8,128)(2,1)} %refs_1_.3), custom_call_target="tpu_custom_call" | custom-call | tf_op jit(solution)/shard_map/exchange_2/pallas_call | solution.py:615
  146.4 1.4 fusion.51
  152.9 2.1 convolution_convert_fusion.3
  156.0 2.3 convolution_convert_fusion.2
  161.5 13.8 %exchange_3.1 = f32[8,512]{1,0:T(8,128)} custom-call(f32[8,512]{1,0:T(8,128)} %select_maximum_fusion.refs_0_), custom_call_target="tpu_custom_call" | custom-call | tf_op jit(solution)/shard_map/exchange_3/pallas_call | solution.py:615
  176.1 2.1 fusion.43
  179.5 1.5 collective-permute-start.3
  183.7 6.0 %depth_back.1 = (f32[2,128,512]{2,1,0:T(8,128)}, f32[2,32,512]{2,1,0:T(8,128)}) custom-call(bf16[2,160,512]{2,1,0:T(8,128)(2,1)} %pad_maximum_fusion.6.padded_ref, bf16[2,16,512]{2,1,0:T(8,128)(2,1)} %copy-done.19, bf16[2,16,512]{2,1,0:T(8,128)(2,1)} %copy-done.20, f32[2,128,512]{2,1,0:T(8,128)} %get-tuple-element.179.ddepth_ref, ...), custom_call_target="tpu_custom_call" | custom-call | tf_op jit(solution)/shard_map/depth_back/pallas_call | solution.py:803
  191.7 1.6 convolution_convert_fusion.6
  195.7 13.1 %attend_back.1 = (bf16[2,128,512]{2,1,0:T(8,128)(2,1)}, bf16[4,2,128,1024]{3,2,1,0:T(8,128)(2,1)}, f32[2,16,512]{2,1,0:T(8,128)}) custom-call(s32[1]{0:T(128)} %bitcast.9.start_ref, s32[2]{0:T(128)} %bitcast.203, f32[2,8]{1,0:T(2,128)} %terms_ref.3, bf16[2,128,512]{2,1,0:T(8,128)(2,1)} %bitcast.144, bf16[4,2,128,1024]{3,2,1,0:T(8,128)(2,1)} %bitcast.136, ...), custom_call_target="tpu_custom_call" | custom-call | tf_op jit(solution)/shard_map/attend_back/pallas_call | solution.py:732
  208.8 58.9 %exchange_4.1 = (bf16[256,1024]{1,0:T(8,128)(2,1)}, f32[64,1024]{1,0:T(8,128)}, f32[64,512]{1,0:T(8,128)}, f32[64,512]{1,0:T(8,128)}, f32[256,512]{1,0:T(8,128)}, /*index=5*/f32[64,2048]{1,0:T(8,128)}) custom-call(bf16[2,2,256,1024]{3,2,1,0:T(8,128)(2,1)} %bitcast.157, bf16[4,2,64,1024]{3,2,1,0:T(8,128)(2,1)} %bitcast.140, ...), custom_call_target="tpu_custom_call" | custom-call | tf_op jit(solution)/shard_map/exchange_4/pallas_call | solution.py:615
  267.7 1.9 multiply_reduce_fusion.2
  272.3 2.1 convolution_convert_fusion.1
  274.4 1.9 convolution_convert_fusion.4
  277.3 2.1 convolution_convert_fusion
  280.4 52.2 %exchange_5.1 = (f32[256,512]{1,0:T(8,128)}, f32[64,2048]{1,0:T(8,128)}, f32[64,1536]{1,0:T(8,128)}, f32[64,256]{1,0:T(8,128)}) custom-call(bf16[4,2,256,512]{3,2,1,0:T(8,128)(2,1)} %bitcast.147, bf16[4,2,64,2048]{3,2,1,0:T(8,128)(2,1)} %bitcast.134, bf16[4,2,64,1536]{3,2,1,0:T(8,128)(2,1)} %bitcast.138, bf16[4,2,64,256]{3,2,1,0:T(8,128)(2,1)} %bitcast.165), custom_call_target="tpu_custom_call" | custom-call | tf_op jit(solution)/shard_map/exchange_5/pallas_call | solution.py:615
  332.7 4.1 %results.1 = (f32[64,2048]{1,0:T(8,128)}, f32[256,512]{1,0:T(8,128)}, f32[64,1536]{1,0:T(8,128)}, f32[64,512]{1,0:T(8,128)}, f32[64,1024]{1,0:T(8,128)}, /*index...) custom-call(f32[64,2048]{1,0:T(8,128)} %get-tuple-element.69.refs_0_, ...), custom_call_target="tpu_custom_call" | custom-call | tf_op jit(solution)/shard_map/results/pallas_call | solution.py:844
  336.8 1.4 copy.74
  (145 shorter events, 48.1 us)
Async XLA Ops:
  0.6 46.5 %copy-start.1 = (bf16[2,1,128,512]{3,2,1,0:T(8,128)(2,1)S(1)}, bf16[2,1,128,512]{3,2,1,0:T(8,128)(2,1)}, u32[]{:S(2)}) copy-start(bf16[2,1,128,512]{3,2,1,0:T(8,128)(2,1)} %param.15) | copy-start | bytes 786436
  47.3 2.5 copy-start.23
  49.8 2.2 copy-start.10
  92.1 8.6 %copy-start.4 = (bf16[8,64,512]{2,1,0:T(8,128)(2,1)S(1)}, bf16[8,64,512]{2,1,0:T(8,128)(2,1)}, u32[]{:S(2)}) copy-start(bf16[8,64,512]{2,1,0:T(8,128)(2,1)} %get-tuple-element.57) | copy-start | bytes 1572868
  92.1 10.3 %copy-start.21 = (s32[2,1]{0,1:T(1,128)S(1)}, s32[2,1]{0,1:T(1,128)}, u32[]{:S(2)}) copy-start(s32[2,1]{0,1:T(1,128)} %param.16) | copy-start | bytes 28
  100.7 1.8 copy-start.12
  102.4 5.5 %copy-start.22 = (pred[32]{0:T(512)(128)(4,1)S(1)}, pred[32]{0:T(512)(128)(4,1)}, u32[]{:S(2)}) copy-start(pred[32]{0:T(512)(128)(4,1)} %constant.45.clone.1) | copy-start | bytes 100
  102.5 6.1 %copy-start.3 = (bf16[2,1,128,512]{3,2,1,0:T(8,128)(2,1)S(1)}, bf16[2,1,128,512]{3,2,1,0:T(8,128)(2,1)}, u32[]{:S(2)}) copy-start(bf16[2,1,128,512]{3,2,1,0:T(8,128)(2,1)} %param.17) | copy-start | bytes 786436
  103.2 5.6 %collective-permute-start.1 = (bf16[2,16,512]{2,1,0:T(8,128)(2,1)S(1)}, bf16[2,16,512]{2,1,0:T(8,128)(2,1)S(1)}, u32[]{:S(2)}, u32[]{:S(2)}) collective-permute-start(bf16[2,16,512]{2,1,0:T(8,128)(2,1)S(1)} %get-tuple-element.192), channel_id=1, source_target_pairs={{1,0},{2,1},{3,2},{5,4},{6,5},{7,6},{9,8},{10,9},{11,10},{13,12},{... | collective-permute-start | bytes 98312 | tf_op jit(solution)/shard_map/ppermute | solution.py:860
  104.5 4.3 %collective-permute-start = (bf16[2,16,512]{2,1,0:T(8,128)(2,1)S(1)}, bf16[2,16,512]{2,1,0:T(8,128)(2,1)S(1)}, u32[]{:S(2)}, u32[]{:S(2)}) collective-permute-start(bf16[2,16,512]{2,1,0:T(8,128)(2,1)S(1)} %get-tuple-element.191), channel_id=1, source_target_pairs={{0,1},{1,2},{2,3},{4,5},{5,6},{6,7},{8,9},{9,10},{10,11},{12,13},{... | collective-permute-start | bytes 98312 | tf_op jit(solution)/shard_map/ppermute | solution.py:859
  144.2 3.8 %copy-start.9 = (bf16[8,64,2048]{2,1,0:T(8,128)(2,1)S(1)}, bf16[8,64,2048]{2,1,0:T(8,128)(2,1)}, u32[]{:S(2)}) copy-start(bf16[8,64,2048]{2,1,0:T(8,128)(2,1)} %get-tuple-element.61) | copy-start | bytes 6291460
  148.0 1.6 copy-start.25
  178.2 3.9 %collective-permute-start.2 = (bf16[2,16,512]{2,1,0:T(8,128)(2,1)S(1)}, bf16[2,16,512]{2,1,0:T(8,128)(2,1)S(1)}, u32[]{:S(2)}, u32[]{:S(2)}) collective-permute-start(bf16[2,16,512]{2,1,0:T(8,128)(2,1)S(1)} %get-tuple-element.190), channel_id=1, source_target_pairs={{0,1},{1,2},{2,3},{4,5},{5,6},{6,7},{8,9},{9,10},{10,11},{12,13},{... | collective-permute-start | bytes 98312 | tf_op jit(solution)/shard_map/ppermute | solution.py:859
  179.5 3.6 %collective-permute-start.3 = (bf16[2,16,512]{2,1,0:T(8,128)(2,1)S(1)}, bf16[2,16,512]{2,1,0:T(8,128)(2,1)S(1)}, u32[]{:S(2)}, u32[]{:S(2)}) collective-permute-start(bf16[2,16,512]{2,1,0:T(8,128)(2,1)S(1)} %get-tuple-element.189), channel_id=1, source_target_pairs={{1,0},{2,1},{3,2},{5,4},{6,5},{7,6},{9,8},{10,9},{11,10},{13,12},{... | collective-permute-start | bytes 98312 | tf_op jit(solution)/shard_map/ppermute | solution.py:860
  189.6 1.4 copy-start.13
  191.0 2.3 copy-start.8
  208.8 58.9 %copy-start.11 = (bf16[8,64,1536]{2,1,0:T(8,128)(2,1)S(1)}, bf16[8,64,1536]{2,1,0:T(8,128)(2,1)}, u32[]{:S(2)}) copy-start(bf16[8,64,1536]{2,1,0:T(8,128)(2,1)} %get-tuple-element.55) | copy-start | bytes 4718596
  208.8 58.9 %copy-start.16 = (bf16[2,128,512]{2,1,0:T(8,128)(2,1)S(1)}, bf16[2,128,512]{2,1,0:T(8,128)(2,1)}, u32[]{:S(2)}) copy-start(bf16[2,128,512]{2,1,0:T(8,128)(2,1)} %get-tuple-element.64) | copy-start | bytes 786436
  267.7 2.2 copy-start.24
  269.6 1.6 copy-start.7
  272.3 2.1 copy-start.15
  274.4 1.9 copy-start.5
  277.2 2.1 copy-start.17
  277.3 2.3 copy-start.18
  (6 other events, 6.6 us)
